TPU v7x, 32 devices: a whole 2x2x4 slice. The times are simulated.
32 devices in a mesh: bricks: 8 (over z, y), group: 4 (over x, core).
Axes of the slice: x: 2, y: 2, z: 4, core: 2. Of those that a mesh axis runs over, the one named last changes fastest.
Arguments:
- right_side: float32 [3, 128, 64, 128], P(None, 'bricks', 'group'), may hold values from -6 to 6
- material: int32 [128, 64, 128], P('bricks', 'group'), may hold values from 0 to 3
- brick_level: int32 [8, 4], P('bricks', 'group'), may hold values from 0 to 2
- mortar_rows: int32 [8, 4, 16], P('bricks', 'group'), may hold values from 0 to 15, each once within a row
- material_mu: float32 [4], replicated, may hold values from 0.5 to 4
- material_lam: float32 [4], replicated, may hold values from 0.25 to 2
- coarse_inverse: float32 [8, 48, 48], P('bricks'), may hold values from -1 to 5, as said below
Outputs:
- solution: float32 [3, 128, 64, 128], P(None, 'bricks', 'group')
- residual: float32 [3, 128, 64, 128], P(None, 'bricks', 'group')
Inputs may be any that keep to these rules, and one draw needn't show every extreme that they name: `coarse_inverse`: each brick row's matrix is of full rank with a positive diagonal.
All inputs are finite; a program needn't handle non-finite values.
Results may differ from a plain program's by a relative error of at most 0.00027.
Values sent between devices are 32-bit elements; how exact they have to be, the bound alone decides.
A program may use at most 64 MiB of HBM per device.

v0:
```python
import functools

import jax
import jax.numpy as jnp
from jax import lax
from jax.experimental import pallas as pl
from jax.experimental.pallas import tpu as pltpu
from jax.sharding import PartitionSpec as P

BLOCK_Z = 32
CHEB = 4
LOW_RATIO = 0.15
BOUND_MARGIN = 1.1
ROUNDS = 2 * CHEB
UNROLL = 4
SWEEP = 7
HIGHEST = lax.Precision.HIGHEST


def kernel(
    nb, ng, dx, dy, dz,
    rhs_in, material_in, level, mortar, mu, lam, inverse_in,
    sol, res, rhs, material, inverse,
    u, r, shear, wx, wyp, wym, wzp, wzm, dg, hb, invd, coef, undo,
    s_send_up, s_send_y, s_recv, above, up_send, y_send, recv,
    m_own, m_all, m2_own, m2_all, c_own, c_all, f_all, inv_recv, pack_send, pack_top, pack_recv, in_sem,
    s_ssem, s_rsem, h_ssem, h_rsem,
    m_ssem, m_rsem, m2_ssem, m2_rsem, c_ssem, c_rsem, p_ssem, p_rsem, i_ssem, i_rsem,
):
    b = lax.axis_index("bricks")
    g = lax.axis_index("group")
    has = [b > 0, b < nb - 1, g > 0, g < ng - 1]
    sends = [has[1], has[0], has[3], has[2]]
    peers = [(b + 1, g), (b - 1, g), (b, g + 1), (b, g - 1)]

    def remote(src, dst, ssem, rsem, peer):
        return pltpu.make_async_remote_copy(
            src_ref=src, dst_ref=dst, send_sem=ssem, recv_sem=rsem,
            device_id=peer, device_id_type=pl.DeviceIdType.MESH,
        )

    barrier = pltpu.get_barrier_semaphore()
    others = [(b, lax.rem(g + k, ng)) for k in range(1, ng)]
    others += [(lax.rem(b + k, nb), g) for k in range(1, nb)]
    around = [(lax.rem(g + k, ng)) for k in range(1, ng)]
    for peer in others:
        pl.semaphore_signal(
            barrier, inc=1, device_id=peer, device_id_type=pl.DeviceIdType.MESH
        )
    for d in range(2):
        @pl.when(has[d])
        def _():
            for at in around:
                pl.semaphore_signal(
                    barrier, inc=1, device_id=(b - 1 + 2 * d, at),
                    device_id_type=pl.DeviceIdType.MESH,
                )

    def fetch(k):
        source = [material_in, rhs_in, inverse_in.at[0]][k]
        return pltpu.make_async_copy(source, [material, rhs, inverse][k], in_sem.at[k])

    for k in range(3):
        fetch(k).start()

    grade = jnp.broadcast_to(level[...], (dy, dz))
    scale = jnp.where(grade == 0, 1.0, jnp.where(grade == 1, 4.0, 16.0))
    zero_face = jnp.zeros((3, dx, dz), jnp.float32)

    order = [mortar[0, 0, k] for k in range(dy)]
    for k in range(dy):
        total = jnp.int32(0)
        for j in range(dy):
            total = jnp.where(order[j] == k, jnp.int32(j), total)
        undo[k] = total

    def lookup(ids, table):
        total = jnp.where(ids == 0, table[0], 0.0)
        for entry in range(1, 4):
            total = jnp.where(ids == entry, table[entry], total)
        return total * scale

    def shear_plane(i, _):
        ids = material[i]
        plane = lookup(ids, mu)
        shear[i + 1] = plane
        hb[i] = lookup(ids, lam)
        s_send_y[0, pl.ds(i, 1), :] = plane[dy - 1 : dy]
        s_send_y[1, pl.ds(i, 1), :] = plane[0:1]
        return 0

    fetch(0).wait()
    lax.fori_loop(0, dx, shear_plane, 0, unroll=UNROLL)
    for k in range(dy):
        s_send_up[k : k + 1, :] = shear[dx, pl.ds(order[k], 1), :]

    both = jnp.where(has[0], len(around), 0) + jnp.where(has[1], len(around), 0)
    pl.semaphore_wait(barrier, len(others) + both)

    def s_copy(d):
        src = [s_send_up, shear.at[1], s_send_y.at[0], s_send_y.at[1]][d]
        return remote(src, s_recv.at[d], s_ssem.at[d], s_rsem.at[d], peers[d])

    def exchange_start(copy, directions=(0, 1, 2, 3)):
        for d in directions:
            @pl.when(sends[d])
            def _():
                copy(d).start()

    def exchange_wait(copy, directions=(0, 1, 2, 3)):
        for d in directions:
            @pl.when(has[d])
            def _():
                copy(d).wait_recv()
        for d in directions:
            @pl.when(sends[d])
            def _():
                copy(d).wait_send()

    exchange_start(s_copy)

    @pl.when(b == 0)
    def _():
        s_recv[0] = shear[1]

    @pl.when(b == nb - 1)
    def _():
        shear[dx + 1] = shear[dx]
        s_recv[1] = shear[dx]

    @pl.when(g == 0)
    def _():
        s_recv[2] = s_send_y[1]

    @pl.when(g == ng - 1)
    def _():
        s_recv[3] = s_send_y[0]

    for d in range(4):
        @pl.when(jnp.logical_not(has[d]))
        def _():
            for turn in range(ROUNDS):
                recv[turn, d] = zero_face
            pack_recv[d] = jnp.zeros(pack_recv.shape[1:], jnp.float32)
            if d < 2:
                inv_recv[d] = jnp.zeros(inv_recv.shape[1:], jnp.float32)
                c_all[2 * d] = jnp.zeros(c_all.shape[1:], jnp.float32)

    fetch(1).wait()
    fetch(2).wait()
    exchange_wait(s_copy)
    shear[0] = s_recv[0]

    @pl.when(b < nb - 1)
    def _():
        for k in range(dy):
            shear[dx + 1, k : k + 1, :] = s_recv[1, pl.ds(undo[k], 1), :]

    row = lax.broadcasted_iota(jnp.int32, (dy, dz), 0)
    lane = lax.broadcasted_iota(jnp.int32, (dy, dz), 1)

    def y_near(v, low, high):
        ym = jnp.where(row == 0, jnp.broadcast_to(low, v.shape), pltpu.roll(v, 1, 0))
        yp = jnp.where(
            row == dy - 1, jnp.broadcast_to(high, v.shape), pltpu.roll(v, dy - 1, 0)
        )
        return ym, yp

    def z_near(v):
        return pltpu.roll(v, 1, 1), pltpu.roll(v, dz - 1, 1)

    def h_copy(turn, slot):
        def copy(d):
            src = [
                up_send.at[turn], u.at[slot, :, 1], y_send.at[turn, 0], y_send.at[turn, 1]
            ][d]
            return remote(
                src, recv.at[turn, d], h_ssem.at[turn, d], h_rsem.at[turn, d], peers[d]
            )
        return copy

    even = lax.rem(b, 2) == 0

    def sweep(plane, turn, slot, carry, unroll, arrive=None):
        if arrive is not None:
            carry = lax.fori_loop(1, dx - 1, plane, carry, unroll=unroll)
            arrive()
        carry = plane(0, carry)
        carry = plane(dx - 1, carry)
        if turn is not None:
            copy = h_copy(turn, slot)

            @pl.when(sends[1] & even)
            def _():
                copy(1).start()

            for c in range(3):
                for k in range(dy):
                    up_send[turn, c, k : k + 1, :] = u[slot, c, dx, pl.ds(order[k], 1), :]
            exchange_start(copy, (0,))

            @pl.when(sends[1] & jnp.logical_not(even))
            def _():
                copy(1).start()

        if arrive is None:
            carry = lax.fori_loop(1, dx - 1, plane, carry, unroll=unroll)
        if turn is not None:
            exchange_start(h_copy(turn, slot), (2, 3))
        return carry

    wx[0] = 0.5 * (shear[0] + shear[1])
    wx[dx] = 0.5 * (shear[dx] + shear[dx + 1])

    def weight_plane(i, best):
        s = shear[i + 1]
        xp = 0.5 * (s + shear[i + 2])
        wx[i + 1] = xp
        xm = 0.5 * (s + shear[i])
        ym, yp = y_near(s, s_recv[2, pl.ds(i, 1), :], s_recv[3, pl.ds(i, 1), :])
        ym = 0.5 * (s + ym)
        yp = 0.5 * (s + yp)
        zm, zp = z_near(s)
        zm = 0.5 * (s + zm)
        zp = 0.5 * (s + zp)
        wyp[i] = yp
        wym[i] = ym
        wzp[i] = jnp.where(lane == dz - 1, 0.0, zp)
        wzm[i] = jnp.where(lane == 0, 0.0, zm)
        total = xp + xm + yp + ym + jnp.where(lane == dz - 1, s, zp) + jnp.where(lane == 0, s, zm)
        bulk = hb[i]
        diagonal = total + 1.5 * bulk
        inv = 1.0 / diagonal
        invd[i] = inv
        dg[i] = total + bulk
        half = 0.5 * bulk
        hb[i] = half
        none = jnp.zeros((1, dz), jnp.float32)
        for d, y in ((2, dy - 1), (3, 0)):
            pack_send[d, 0, pl.ds(i, 1), :] = inv[y : y + 1]
            pack_send[d, 1, pl.ds(i, 1), :] = half[y : y + 1]
            first, last = isinstance(i, int) and i == 0, isinstance(i, int) and i == dx - 1
            pack_send[d, 2, pl.ds(i, 1), :] = xm[y : y + 1] if first else none
            pack_send[d, 3, pl.ds(i, 1), :] = xp[y : y + 1] if last else none
        if isinstance(i, int):
            planes = (inv, half, jnp.where(row == 0, ym, 0.0), jnp.where(row == dy - 1, yp, 0.0))
            for k, value in enumerate(planes):
                if i == 0:
                    pack_send[1, k] = value
                else:
                    pack_top[k] = value
        for c in range(3):
            d0 = rhs[c, i] * inv
            u[0, c, i + 1] = d0
            y_send[0, 0, c, pl.ds(i, 1), :] = d0[dy - 1 : dy]
            y_send[0, 1, c, pl.ds(i, 1), :] = d0[0:1]
        return jnp.maximum(best, (2.0 * total + 2.5 * bulk) / diagonal)

    best = sweep(weight_plane, 0, 0, jnp.zeros((dy, dz), jnp.float32), 2)
    m_own[...] = jnp.broadcast_to(jnp.max(best, axis=0, keepdims=True), m_own.shape)

    def halo_wait(turn, slot):
        exchange_wait(h_copy(turn, slot))
        place_halo(turn, slot)

    def x_arrival(turn, slot):
        def arrive():
            exchange_wait(h_copy(turn, slot), (0, 1))
            place_halo(turn, slot)
        return arrive

    def place_halo(turn, slot):
        for c in range(3):
            u[slot, c, 0] = recv[turn, 0, c]
            above[c] = recv[turn, 1, c]
        for c in range(3):
            for k in range(dy):
                u[slot, c, dx + 1, k : k + 1, :] = above[c, pl.ds(undo[k], 1), :]

    def apply_plane(i, slot, low, high):
        v = [u[slot, c, i + 1] for c in range(3)]
        coupled = hb[i] * (v[0] + v[1] + v[2])
        out = []
        for c in range(3):
            ym, yp = y_near(v[c], low(c, i), high(c, i))
            zm, zp = z_near(v[c])
            near = wx[i] * u[slot, c, i] + wx[i + 1] * u[slot, c, i + 2]
            near = near + wym[i] * ym + wyp[i] * yp + wzm[i] * zm + wzp[i] * zp
            out.append(dg[i] * v[c] + coupled - near)
        return v, out

    def recv_rows(turn):
        return (
            lambda c, i: recv[turn, 2, c, pl.ds(i, 1), :],
            lambda c, i: recv[turn, 3, c, pl.ds(i, 1), :],
        )

    def bcoef(k):
        return jnp.broadcast_to(coef[k : k + 1, :], (dy, dz))

    def ring_start(own, store, ssem, rsem, peer_of, count, mine):
        copies = []
        for k in range(1, count):
            copies.append(remote(own, store.at[k], ssem.at[k], rsem.at[k], peer_of(k)))
        for copy in copies:
            copy.start()
        return copies

    group_peer = lambda k: (b, lax.rem(g + k, ng))
    brick_peer = lambda k: (lax.rem(b + k, nb), g)

    m_copies = ring_start(m_own, m_all, m_ssem, m_rsem, group_peer, ng, g)
    halo_wait(0, 0)

    low, high = recv_rows(0)

    def first_plane(i, _):
        _, out = apply_plane(i, 0, low, high)
        inv = invd[i]
        for c in range(3):
            r[c, i] = out[c]
            q = out[c] * inv
            u[1, c, i + 1] = q
            y_send[1, 0, c, pl.ds(i, 1), :] = q[dy - 1 : dy]
            y_send[1, 1, c, pl.ds(i, 1), :] = q[0:1]
        return 0

    sweep(first_plane, 1, 1, 0, SWEEP)

    def p_copy(d):
        return remote(
            pack_send.at[d], pack_recv.at[d], p_ssem.at[d], p_rsem.at[d], peers[d]
        )

    for q in range(4):
        for k in range(dy):
            pack_send[0, q, k : k + 1, :] = pack_top[q, pl.ds(order[k], 1), :]
    top = m_own[...]
    for k, copy in enumerate(m_copies):
        copy.wait()
        top = jnp.maximum(top, m_all[k + 1])
    m2_own[...] = top
    m2_copies = ring_start(m2_own, m2_all, m2_ssem, m2_rsem, brick_peer, nb, b)
    exchange_start(p_copy)
    halo_wait(1, 1)
    for k, copy in enumerate(m2_copies):
        copy.wait()
        top = jnp.maximum(top, m2_all[k + 1])
    upper = BOUND_MARGIN * jnp.broadcast_to(jnp.max(top, axis=1, keepdims=True), top.shape)
    lower = LOW_RATIO * upper
    theta = 0.5 * (upper + lower)
    delta = 0.5 * (upper - lower)
    sigma = theta / delta
    damping = 1.0 / sigma
    inv_theta = 1.0 / theta
    coef[0:8] = inv_theta
    rows = []
    for turn in range(1, CHEB):
        following = 1.0 / (2.0 * sigma - damping)
        rows.append((following * damping, 2.0 * following / delta))
        damping = following
    for turn, (a, c2) in enumerate(rows):
        coef[8 + 2 * turn : 9 + 2 * turn] = a[0:1]
        coef[9 + 2 * turn : 10 + 2 * turn] = c2[0:1]
    coef[14:15] = (rows[0][0] * inv_theta + rows[0][1])[0:1]
    coef[15:16] = (rows[0][1] * inv_theta)[0:1]

    alpha, beta, it = bcoef(14), bcoef(15), bcoef(0)

    def combine_plane(i, _):
        for c in range(3):
            d0 = u[0, c, i + 1]
            sol[c, i] = d0 * it
            res[c, i] = rhs[c, i] - r[c, i] * it
            u[0, c, i + 1] = alpha * d0 - beta * u[1, c, i + 1]
        return 0

    lax.fori_loop(0, dx, combine_plane, 0, unroll=UNROLL)
    for c in range(3):
        for p in (0, dx + 1):
            u[0, c, p] = alpha * u[0, c, p] - beta * u[1, c, p]
        for d in (2, 3):
            recv[1, d, c] = alpha[:dx] * recv[0, d, c] - beta[:dx] * recv[1, d, c]

    def step(slot, low, high, a, c2, following, summed=False, send=True, arrive=None):
        other = 1 - slot

        def plane(i, sums):
            v, out = apply_plane(i, slot, low, high)
            inv = invd[i]
            new = []
            for c in range(3):
                rest = res[c, i] - out[c]
                res[c, i] = rest
                sol[c, i] = sol[c, i] + v[c]
                if summed:
                    new.append(sums[c] + rest)
                if following is None:
                    continue
                ahead = c2 * (rest * inv)
                if a is not None:
                    ahead = ahead + a * v[c]
                u[other, c, i + 1] = ahead
                if not send:
                    continue
                y_send[following, 0, c, pl.ds(i, 1), :] = ahead[dy - 1 : dy]
                y_send[following, 1, c, pl.ds(i, 1), :] = ahead[0:1]
            return tuple(new)

        init = ()
        if summed:
            init = tuple(jnp.zeros((dy, dz), jnp.float32) for _ in range(3))
        return sweep(plane, following if send else None, other, init, SWEEP, arrive)

    def i_copy(d):
        return remote(inverse, inv_recv.at[d], i_ssem.at[d], i_rsem.at[d], peers[d])

    slot = 0
    for turn in range(1, CHEB):
        low, high = recv_rows(turn)
        if turn + 1 < CHEB:
            step(slot, low, high, bcoef(8 + 2 * turn), bcoef(9 + 2 * turn), turn + 1)
            slot = 1 - slot
            if turn == 1:
                exchange_start(i_copy, (0, 1))
            if turn + 2 < CHEB:
                halo_wait(turn + 1, slot)
            else:
                exchange_wait(h_copy(turn + 1, slot), (2, 3))
        else:
            sums = step(
                slot, low, high, None, bcoef(0), CHEB, summed=True, arrive=x_arrival(turn, slot)
            )

    c_own[...] = jnp.zeros(c_own.shape, jnp.float32)
    for c in range(3):
        c_own[c : c + 1, :] = jnp.sum(sums[c], axis=0, keepdims=True)
    c_all[1, g] = c_own[...]

    def c_copy(q, k):
        slot = q * ng + k
        return remote(
            c_own, c_all.at[q, g], c_ssem.at[slot], c_rsem.at[slot],
            (b + 1 - q, lax.rem(g + k, ng)),
        )

    def c_arrival(q, k):
        slot = q * ng + k
        source = lax.rem(g + ng - k, ng)
        return remote(
            c_own, c_all.at[q, source], c_ssem.at[slot], c_rsem.at[slot],
            (b + 1 - q, lax.rem(g + k, ng)),
        )

    def coarse_all(to_do, flags):
        for q in (0, 2, 1):
            first = 1 if q == 1 else 0
            if q == 1:
                for k in range(first, ng):
                    to_do(q, k)
                continue

            @pl.when(flags[q])
            def _():
                for k in range(first, ng):
                    to_do(q, k)

    coarse_all(lambda q, k: c_copy(q, k).start(), {0: has[1], 2: has[0]})
    f_all[...] = jnp.zeros(f_all.shape, jnp.float32)
    exchange_wait(p_copy)
    exchange_wait(i_copy, (0, 1))
    coarse_all(lambda q, k: c_arrival(q, k).wait_recv(), {0: has[0], 2: has[1]})
    coarse_all(lambda q, k: c_copy(q, k).wait_send(), {0: has[1], 2: has[0]})

    cells_z = dz // BLOCK_Z
    size = 3 * cells_z * ng
    flat = c_all[...].reshape(3 * ng * 8, dz)
    li = lax.broadcasted_iota(jnp.int32, (dz, size), 0)
    ki = lax.broadcasted_iota(jnp.int32, (dz, size), 1)
    gather = jnp.where(li // BLOCK_Z == ki % cells_z, 1.0 / (dx * dy * BLOCK_Z), 0.0)
    spread = jnp.dot(flat, gather, precision=HIGHEST, preferred_element_type=jnp.float32)
    ri = lax.broadcasted_iota(jnp.int32, (ng * 8, size), 0)
    kk = lax.broadcasted_iota(jnp.int32, (ng * 8, size), 1) // cells_z
    mine = (ri // 8 == kk // 3) & (ri % 8 == kk % 3)
    bi = lax.broadcasted_iota(jnp.int32, (size, dz), 0)
    bl = lax.broadcasted_iota(jnp.int32, (size, dz), 1)
    placed = bi % cells_z == bl // BLOCK_Z
    for q in range(3):
        part = spread[q * ng * 8 : (q + 1) * ng * 8]
        vector = jnp.sum(jnp.where(mine, part, 0.0), axis=0, keepdims=True)
        matrix = inverse[...] if q == 1 else inv_recv[q // 2]
        correction = jnp.sum(matrix * vector, axis=1, keepdims=True)
        table = jnp.where(placed, jnp.broadcast_to(correction, (size, dz)), 0.0)
        for k in range(ng):
            for c in range(3):
                start = (k * 3 + c) * cells_z
                f_all[q, k + 1, c : c + 1, :] = jnp.sum(
                    table[start : start + cells_z], axis=0, keepdims=True
                )

    def full(q, at, c):
        return jnp.broadcast_to(f_all[q, at, c : c + 1, :], (dy, dz))

    own_fine = [full(1, g + 1, c) for c in range(3)]

    def fill_plane(i, _):
        for c in range(3):
            u[0, c, i + 1] = own_fine[c]
        return 0

    lax.fori_loop(0, dx, fill_plane, 0, unroll=UNROLL)
    for c in range(3):
        u[0, c, 0] = full(0, g + 1, c)
        u[0, c, dx + 1] = full(2, g + 1, c)
    it = bcoef(0)
    exchange_wait(h_copy(CHEB, 1))
    step(
        0,
        lambda c, i: f_all[1, g, c : c + 1, :],
        lambda c, i: f_all[1, g + 2, c : c + 1, :],
        None,
        it,
        CHEB,
        send=False,
    )

    def fine_on_face(d, near, cross, here, before, after):
        inv, half, w_low, w_high = [pack_recv[d, k] for k in range(4)]
        zm, zp = z_near(near)
        zm = jnp.where(lane == 0, 0.0, 0.5 * (near + zm))
        zp = jnp.where(lane == dz - 1, 0.0, 0.5 * (near + zp))
        rim = jnp.where((lane == 0) | (lane == dz - 1), near, 0.0)
        weight = 2.0 * half + cross + w_low + w_high + zm + zp + rim
        values = [full(*here, c) for c in range(3)]
        coupled = half * (values[0] + values[1] + values[2])
        for c in range(3):
            fm, fp = z_near(values[c])
            applied = weight * values[c] + coupled - cross * own_fine[c]
            applied = applied - zm * fm - zp * fp
            applied = applied - w_low * full(*before, c) - w_high * full(*after, c)
            recv[CHEB, d, c] = recv[CHEB, d, c] - it * (inv * applied)

    fine_on_face(0, s_recv[0], wx[0], (0, g + 1), (0, g), (0, g + 2))
    fine_on_face(1, s_recv[1], 0.5 * (s_recv[1] + s_send_up[...]), (2, g + 1), (2, g), (2, g + 2))
    fine_on_face(2, s_recv[2], 0.5 * (s_recv[2] + s_send_y[1]), (1, g), (0, g), (2, g))
    fine_on_face(3, s_recv[3], 0.5 * (s_recv[3] + s_send_y[0]), (1, g + 2), (0, g + 2), (2, g + 2))
    place_halo(CHEB, 1)

    slot = 1
    for turn in range(CHEB):
        if turn + 1 == CHEB:
            exchange_wait(h_copy(CHEB + turn, slot), (2, 3))
        elif turn > 0:
            halo_wait(CHEB + turn, slot)
        low, high = recv_rows(CHEB + turn)
        if turn + 1 < CHEB:
            step(slot, low, high, bcoef(8 + 2 * turn), bcoef(9 + 2 * turn), CHEB + turn + 1)
            slot = 1 - slot
        else:
            step(
                slot, low, high, None, None, None, arrive=x_arrival(CHEB + turn, slot)
            )


def per_device(rhs, material, level, mortar, mu, lam, inverse):
    nb = lax.axis_size("bricks")
    ng = lax.axis_size("group")
    dx, dy, dz = material.shape
    f32 = jnp.float32
    vmem = pl.BlockSpec(memory_space=pltpu.VMEM)
    smem = pl.BlockSpec(memory_space=pltpu.SMEM)
    hbm = pl.BlockSpec(memory_space=pltpu.HBM)
    dma = pltpu.SemaphoreType.DMA
    grid = pltpu.VMEM((dx, dy, dz), f32)
    cg = inverse.shape[1]
    scratch = [
        pltpu.VMEM((3, dx, dy, dz), f32),
        pltpu.VMEM((dx, dy, dz), jnp.int32),
        pltpu.VMEM((cg, cg), f32),
        pltpu.VMEM((2, 3, dx + 2, dy, dz), f32),
        pltpu.VMEM((3, dx, dy, dz), f32),
        pltpu.VMEM((dx + 2, dy, dz), f32),
        pltpu.VMEM((dx + 1, dy, dz), f32),
        grid, grid, grid, grid, grid, grid, grid,
        pltpu.VMEM((16, dz), f32),
        pltpu.SMEM((dy,), jnp.int32),
        pltpu.VMEM((dy, dz), f32),
        pltpu.VMEM((2, dx, dz), f32),
        pltpu.VMEM((4, dx, dz), f32),
        pltpu.VMEM((3, dy, dz), f32),
        pltpu.VMEM((ROUNDS, 3, dy, dz), f32),
        pltpu.VMEM((ROUNDS, 2, 3, dx, dz), f32),
        pltpu.VMEM((ROUNDS, 4, 3, dx, dz), f32),
        pltpu.VMEM((8, dz), f32),
        pltpu.VMEM((ng, 8, dz), f32),
        pltpu.VMEM((8, dz), f32),
        pltpu.VMEM((nb, 8, dz), f32),
        pltpu.VMEM((8, dz), f32),
        pltpu.VMEM((3, ng, 8, dz), f32),
        pltpu.VMEM((3, ng + 2, 8, dz), f32),
        pltpu.VMEM((2, cg, cg), f32),
        pltpu.VMEM((4, 4, dx, dz), f32),
        pltpu.VMEM((4, dy, dz), f32),
        pltpu.VMEM((4, 4, dx, dz), f32),
        dma((3,)),
        dma((4,)), dma((4,)),
        dma((ROUNDS, 4)), dma((ROUNDS, 4)),
        dma((ng,)), dma((ng,)),
        dma((nb,)), dma((nb,)),
        dma((3 * ng,)), dma((3 * ng,)),
        dma((4,)), dma((4,)),
        dma((2,)), dma((2,)),
    ]
    rhs, material, inverse, mortar, mu, lam = (
        pltpu.with_memory_space_constraint(x, pltpu.HBM)
        for x in (rhs, material, inverse, mortar, mu, lam)
    )
    return pl.pallas_call(
        functools.partial(kernel, nb, ng, dx, dy, dz),
        out_shape=(
            jax.ShapeDtypeStruct(rhs.shape, f32),
            jax.ShapeDtypeStruct(rhs.shape, f32),
        ),
        in_specs=[hbm, hbm, vmem, smem, smem, smem, hbm],
        out_specs=(vmem, vmem),
        scratch_shapes=scratch,
        compiler_params=pltpu.CompilerParams(
            collective_id=0, has_side_effects=True, vmem_limit_bytes=16 * 2**20
        ),
    )(rhs, material, level, mortar, mu, lam, inverse)


def solution(mesh):
    return jax.shard_map(
        per_device,
        mesh=mesh,
        in_specs=(
            P(None, "bricks", "group", None),
            P("bricks", "group", None),
            P("bricks", "group"),
            P("bricks", "group", None),
            P(),
            P(),
            P("bricks", None, None),
        ),
        out_specs=(P(None, "bricks", "group", None), P(None, "bricks", "group", None)),
        check_vma=False,
    )
```

profile of v0, /device:TPU:0, one launch (start us, length us, event | category | flops | bytes accessed | tf_op | source)
XLA Modules:
  0.0 43.2 jit_solution(2242505583547775215)
XLA Ops:
  1.3 40.4 %shard_map.86 = (f32[3,16,16,128]{3,2,1,0:T(8,128)S(1)}, f32[3,16,16,128]{3,2,1,0:T(8,128)S(1)}) custom-call(f32[3,16,16,128]{3,2,1,0:T(8,128)} %rhs_in.1, s32[16,16,128]{2,1,0:T(8,128)} %material_in.1, s32[1,1]{1,0:T(1,128)S(6)} %copy.11.level, s32[1,1,16]{2,1,0:T(1,128)} %mortar.1, f32[4]{0:T(128)} %mu.1, f32[4]{0:T(128)} %lam.1, f32[1,48,48]{2,1,0:T(8,128)} %inverse_in.1), custom_call_target="tpu_custom_call" | custom-call | tf_op jit(solution)/shard_map/pallas_call | solution.py:618
  41.7 0.7 %copy.12 = f32[3,16,16,128]{3,2,1,0:T(8,128)} copy(f32[3,16,16,128]{3,2,1,0:T(8,128)S(1)} %get-tuple-element.4) | data formatting | bytes 786432
  42.4 0.7 %copy.13 = f32[3,16,16,128]{3,2,1,0:T(8,128)} copy(f32[3,16,16,128]{3,2,1,0:T(8,128)S(1)} %get-tuple-element.5) | data formatting | bytes 786432
where the time goes:
time: 43.3 us; the launch traced here: 43.2 us
  Pallas kernels  40.4 us (93%)
  local copies, waits for them, and re-layouts  1.49 us (3%)
  between operations  1.29 us (3%)
    pallas_call x1, Pallas kernels, per_device(): pl.pallas_call(functools.partial(kernel, nb, ng, dx, dy, dz), out_shape=(...  40.4 us
    unnamed x2, local copies, waits for them, and re-layouts  1.49 us

commit v1 on v0

v1 whole, which is shorter than its diff:
```python
import functools

import jax
import jax.numpy as jnp
from jax import lax
from jax.experimental import pallas as pl
from jax.experimental.pallas import tpu as pltpu
from jax.sharding import PartitionSpec as P

BLOCK_Z = 32
CHEB = 4
LOW_RATIO = 0.15
BOUND_MARGIN = 1.1
ROUNDS = 5
DEPTH = (2, 2, 1, 2, 1)
UNROLL = 4
SWEEP = 7
INNER = 6
HIGHEST = lax.Precision.HIGHEST


def kernel(
    nb, ng, dx, dy, dz,
    rhs_in, material_in, level, mortar, mu, lam, inverse_in,
    sol, res, rhs, material, inverse,
    u, r, shear, wx, wyp, wym, wzp, wzm, dg, hb, invd, coef,
    s_send_up, s_send_y, s_recv, static_send, static_recv, index_send, index_recv, index,
    faces, mixed, y_send, corner_send, recv_x, recv_y, recv_d, ghost, gy, before,
    m_own, m_all, m2_own, m2_all, c_own, c_all, f_all, inv_recv, in_sem,
    s_ssem, s_rsem, t_ssem, t_rsem, h_ssem, h_rsem,
    m_ssem, m_rsem, m2_ssem, m2_rsem, c_ssem, c_rsem, i_ssem, i_rsem,
):
    b = lax.axis_index("bricks")
    g = lax.axis_index("group")
    has = [b > 0, b < nb - 1, g > 0, g < ng - 1]
    sends = [has[1], has[0], has[3], has[2]]
    peers = [(b + 1, g), (b - 1, g), (b, g + 1), (b, g - 1)]
    corners = [(0, 0), (0, 1), (1, 0), (1, 1)]
    has_corner = [has[sx] & has[2 + sy] for sx, sy in corners]
    corner_peer = [(b + 2 * sx - 1, g + 2 * sy - 1) for sx, sy in corners]

    def remote(src, dst, ssem, rsem, peer):
        return pltpu.make_async_remote_copy(
            src_ref=src, dst_ref=dst, send_sem=ssem, recv_sem=rsem,
            device_id=peer, device_id_type=pl.DeviceIdType.MESH,
        )

    barrier = pltpu.get_barrier_semaphore()
    others = [(b, lax.rem(g + k, ng)) for k in range(1, ng)]
    others += [(lax.rem(b + k, nb), g) for k in range(1, nb)]
    around = [(lax.rem(g + k, ng)) for k in range(1, ng)]
    for peer in others:
        pl.semaphore_signal(
            barrier, inc=1, device_id=peer, device_id_type=pl.DeviceIdType.MESH
        )
    for d in range(2):
        @pl.when(has[d])
        def _():
            for at in around:
                pl.semaphore_signal(
                    barrier, inc=1, device_id=(b - 1 + 2 * d, at),
                    device_id_type=pl.DeviceIdType.MESH,
                )

    def fetch(k):
        source = [material_in, rhs_in, inverse_in.at[0]][k]
        return pltpu.make_async_copy(source, [material, rhs, inverse][k], in_sem.at[k])

    for k in range(3):
        fetch(k).start()

    row = lax.broadcasted_iota(jnp.int32, (dy, dz), 0)
    lane = lax.broadcasted_iota(jnp.int32, (dy, dz), 1)
    grade = jnp.broadcast_to(level[...], (dy, dz))
    scale = jnp.where(grade == 0, 1.0, jnp.where(grade == 1, 4.0, 16.0))
    zero_face = jnp.zeros((dy, dz), jnp.float32)

    order = [mortar[0, 0, k] for k in range(dy)]
    order_here = jnp.zeros((dy, dz), jnp.int32)
    undo_here = jnp.zeros((dy, dz), jnp.int32)
    for k in range(dy):
        order_here = jnp.where(row == k, order[k], order_here)
        undo_here = jnp.where(row == order[k], k, undo_here)
    index_send[...] = order_here
    index[0] = order_here
    index[1] = undo_here

    def permute(value, k):
        half = dy // 2
        parts = []
        for h in range(2):
            at = index[k, h * half : (h + 1) * half]
            within = jnp.bitwise_and(at, half - 1)
            low = jnp.take_along_axis(value[:half], within, axis=0)
            high = jnp.take_along_axis(value[half:], within, axis=0)
            parts.append(jnp.where(at < half, low, high))
        return jnp.concatenate(parts, axis=0)

    def lookup(ids, table):
        total = jnp.where(ids == 0, table[0], 0.0)
        for entry in range(1, 4):
            total = jnp.where(ids == entry, table[entry], total)
        return total * scale

    def shear_plane(i, _):
        ids = material[i]
        plane = lookup(ids, mu)
        bulk = lookup(ids, lam)
        shear[i + 1] = plane
        hb[i] = bulk
        s_send_y[0, pl.ds(i, 1), :] = plane[dy - 1 : dy]
        s_send_y[1, pl.ds(i, 1), :] = plane[0:1]
        for d, near, far in ((2, dy - 1, dy - 2), (3, 0, 1)):
            static_send[d, 0, pl.ds(i, 1), :] = plane[near : near + 1]
            static_send[d, 1, pl.ds(i, 1), :] = plane[far : far + 1]
            static_send[d, 2, pl.ds(i, 1), :] = bulk[near : near + 1]
        return 0

    fetch(0).wait()
    lax.fori_loop(0, dx, shear_plane, 0, unroll=UNROLL)
    s_send_up[...] = permute(shear[dx], 0)
    for d, near, far in ((0, dx - 1, dx - 2), (1, 0, 1)):
        static_send[d, 0] = shear[near + 1]
        static_send[d, 1] = shear[far + 1]
        static_send[d, 2] = hb[near]

    both = jnp.where(has[0], len(around), 0) + jnp.where(has[1], len(around), 0)
    pl.semaphore_wait(barrier, len(others) + both)

    def s_copy(d):
        src = [s_send_up, shear.at[1], s_send_y.at[0], s_send_y.at[1]][d]
        return remote(src, s_recv.at[d], s_ssem.at[d], s_rsem.at[d], peers[d])

    def t_copy(d):
        if d == 4:
            return remote(index_send, index_recv, t_ssem.at[4], t_rsem.at[4], peers[0])
        return remote(
            static_send.at[d], static_recv.at[d], t_ssem.at[d], t_rsem.at[d], peers[d]
        )

    def exchange_start(copy, directions=(0, 1, 2, 3)):
        for d in directions:
            @pl.when(sends[d % 4])
            def _():
                copy(d).start()

    def arrive_wait(copy, directions=(0, 1, 2, 3)):
        for d in directions:
            @pl.when(has[d % 4])
            def _():
                copy(d).wait_recv()

    def sent_wait(copy, directions=(0, 1, 2, 3)):
        for d in directions:
            @pl.when(sends[d % 4])
            def _():
                copy(d).wait_send()

    def exchange_wait(copy, directions=(0, 1, 2, 3)):
        arrive_wait(copy, directions)
        sent_wait(copy, directions)

    exchange_start(s_copy)
    exchange_start(t_copy, (4, 0, 1, 2, 3))

    @pl.when(b == 0)
    def _():
        s_recv[0] = shear[1]
        index_recv[...] = row

    @pl.when(b == nb - 1)
    def _():
        s_recv[1] = shear[dx]

    @pl.when(g == 0)
    def _():
        s_recv[2] = s_send_y[1]

    @pl.when(g == ng - 1)
    def _():
        s_recv[3] = s_send_y[0]

    for d in range(4):
        @pl.when(jnp.logical_not(has[d]))
        def _():
            one = jnp.ones((dy, dz), jnp.float32)
            for k in range(3):
                static_recv[d, k] = one
            for turn in range(ROUNDS):
                for c in range(3):
                    for j in range(2):
                        if d < 2:
                            recv_x[turn, d, c, j] = zero_face
                        else:
                            recv_y[turn, d - 2, j, c] = zero_face
            if d < 2:
                inv_recv[d] = jnp.zeros(inv_recv.shape[1:], jnp.float32)
                c_all[2 * d] = jnp.zeros(c_all.shape[1:], jnp.float32)

    for k in range(4):
        @pl.when(jnp.logical_not(has_corner[k]))
        def _():
            for turn in range(ROUNDS):
                if DEPTH[turn] == 2:
                    recv_d[turn, k] = jnp.zeros(recv_d.shape[2:], jnp.float32)

    fetch(1).wait()
    fetch(2).wait()
    exchange_wait(s_copy)
    shear[0] = s_recv[0]

    @pl.when(b < nb - 1)
    def _():
        shear[dx + 1] = permute(s_recv[1], 1)

    @pl.when(b == nb - 1)
    def _():
        shear[dx + 1] = shear[dx]

    def rows_near(v, low, high):
        m = jnp.where(row == 0, jnp.broadcast_to(low, v.shape), pltpu.roll(v, 1, 0))
        p = jnp.where(
            row == dy - 1, jnp.broadcast_to(high, v.shape), pltpu.roll(v, dy - 1, 0)
        )
        return m, p

    def z_near(v):
        return pltpu.roll(v, 1, 1), pltpu.roll(v, dz - 1, 1)

    def h_copy(turn, slot):
        deep = DEPTH[turn]

        def copy(d):
            if d == 0:
                src = u.at[slot, :, dx + 1 - deep : dx + 1]
                dst = recv_x.at[turn, 0, :, 2 - deep : 2]
            elif d == 1:
                src = u.at[slot, :, 1 : 1 + deep]
                dst = recv_x.at[turn, 1, :, 0:deep]
            else:
                src = y_send.at[turn, d - 2, 0:deep]
                dst = recv_y.at[turn, d - 2, 0:deep]
            return remote(src, dst, h_ssem.at[turn, d], h_rsem.at[turn, d], peers[d])
        return copy

    def corner_copy(turn, k):
        return remote(
            corner_send.at[turn, k], recv_d.at[turn, 3 - k],
            h_ssem.at[turn, 4 + k], h_rsem.at[turn, 7 - k], corner_peer[k],
        )

    def corner_arrival(turn, k):
        return remote(
            corner_send.at[turn, k], recv_d.at[turn, k],
            h_ssem.at[turn, 4 + k], h_rsem.at[turn, 4 + k], corner_peer[k],
        )

    even = lax.rem(b, 2) == 0

    def send_faces(turn, slot):
        copy = h_copy(turn, slot)

        @pl.when(sends[1] & even)
        def _():
            copy(1).start()

        exchange_start(copy, (0,))

        @pl.when(sends[1] & jnp.logical_not(even))
        def _():
            copy(1).start()

        if DEPTH[turn] == 1:
            return
        for c in range(3):
            bottom, top = u[slot, c, 1], u[slot, c, dx]
            mixed_low, mixed_high = permute(bottom, 3), permute(top, 0)
            mixed[0, c] = mixed_low
            mixed[1, c] = mixed_high
            for k, (sx, sy) in enumerate(corners):
                y = (dy - 1) * sy
                plane, other = ((bottom, mixed_low), (top, mixed_high))[sx]
                corner_send[turn, k, c : c + 1, :] = plane[y : y + 1]
                corner_send[turn, k, 3 + c : 4 + c, :] = other[y : y + 1]
        for k in range(4):
            @pl.when(has_corner[k])
            def _():
                corner_copy(turn, k).start()

    def send_rows(turn, slot):
        exchange_start(h_copy(turn, slot), (2, 3))

    def store_rows(turn, c, i, value):
        y_send[turn, 0, 0, c, pl.ds(i, 1), :] = value[dy - 1 : dy]
        y_send[turn, 1, 0, c, pl.ds(i, 1), :] = value[0:1]
        if DEPTH[turn] == 2:
            y_send[turn, 0, 1, c, pl.ds(i, 1), :] = value[dy - 2 : dy - 1]
            y_send[turn, 1, 1, c, pl.ds(i, 1), :] = value[1:2]

    def corners_wait(turn):
        for k in range(4):
            @pl.when(has_corner[k])
            def _():
                corner_arrival(turn, k).wait_recv()
        for k in range(4):
            @pl.when(has_corner[k])
            def _():
                corner_copy(turn, k).wait_send()

    def nearest(turn, s, c):
        return recv_x[turn, s, c, 1 - s]

    def place_faces(turn, slot):
        for c in range(3):
            u[slot, c, 0] = permute(nearest(turn, 0, c), 2)
            u[slot, c, dx + 1] = permute(nearest(turn, 1, c), 1)

    def sweep_send(plane, turn, slot, carry):
        deep = DEPTH[turn]
        for i in range(deep):
            carry = plane(i, carry)
            carry = plane(dx - 1 - i, carry)
        send_faces(turn, slot)
        unroll = INNER if deep == 2 else SWEEP
        carry = lax.fori_loop(deep, dx - deep, plane, carry, unroll=unroll)
        send_rows(turn, slot)
        return carry

    def sweep_receive(plane, turn, slot, carry, faces_done=None):
        exchange_wait(h_copy(turn, slot), (2, 3))
        carry = lax.fori_loop(1, dx - 1, plane, carry, unroll=SWEEP)
        exchange_wait(h_copy(turn, slot), (0, 1))
        if DEPTH[turn] == 2:
            corners_wait(turn)
        place_faces(turn, slot)
        if faces_done is not None:
            faces_done()
        carry = plane(0, carry)
        carry = plane(dx - 1, carry)
        return carry

    wx[0] = 0.5 * (shear[0] + shear[1])
    wx[dx] = 0.5 * (shear[dx] + shear[dx + 1])

    exchange_wait(t_copy, (4,))
    index[2] = index_recv[...]
    undo_below = jnp.zeros((dy, dz), jnp.int32)
    for k in range(dy):
        at = jnp.broadcast_to(index_recv[k : k + 1, :], (dy, dz))
        undo_below = jnp.where(row == at, k, undo_below)
    index[3] = undo_below

    def weight_plane(i, best):
        s = shear[i + 1]
        xp = 0.5 * (s + shear[i + 2])
        wx[i + 1] = xp
        xm = 0.5 * (s + shear[i])
        ym, yp = rows_near(s, s_recv[2, pl.ds(i, 1), :], s_recv[3, pl.ds(i, 1), :])
        ym = 0.5 * (s + ym)
        yp = 0.5 * (s + yp)
        zm, zp = z_near(s)
        zm = 0.5 * (s + zm)
        zp = 0.5 * (s + zp)
        wyp[i] = yp
        wym[i] = ym
        wzp[i] = jnp.where(lane == dz - 1, 0.0, zp)
        wzm[i] = jnp.where(lane == 0, 0.0, zm)
        total = xp + xm + yp + ym + jnp.where(lane == dz - 1, s, zp) + jnp.where(lane == 0, s, zm)
        bulk = hb[i]
        diagonal = total + 1.5 * bulk
        inv = 1.0 / diagonal
        invd[i] = inv
        dg[i] = total + bulk
        hb[i] = 0.5 * bulk
        for c in range(3):
            d0 = rhs[c, i] * inv
            u[0, c, i + 1] = d0
            store_rows(0, c, i, d0)
        return jnp.maximum(best, (2.0 * total + 2.5 * bulk) / diagonal)

    below_shear = permute(shear[1], 3)
    faces[0] = below_shear
    for k, (sx, sy) in enumerate(corners):
        y = (dy - 1) * sy
        plane = shear[(1, dx)[sx]]
        other = (below_shear, s_send_up[...])[sx]
        corner_send[0, k, 6:7, :] = plane[y : y + 1]
        corner_send[0, k, 7:8, :] = other[y : y + 1]

    best = sweep_send(weight_plane, 0, 0, jnp.zeros((dy, dz), jnp.float32))
    m_own[...] = jnp.broadcast_to(jnp.max(best, axis=0, keepdims=True), m_own.shape)

    def apply_plane(i, slot, low, high):
        v = [u[slot, c, i + 1] for c in range(3)]
        coupled = hb[i] * (v[0] + v[1] + v[2])
        out = []
        for c in range(3):
            ym, yp = rows_near(v[c], low(c, i), high(c, i))
            zm, zp = z_near(v[c])
            near = wx[i] * u[slot, c, i] + wx[i + 1] * u[slot, c, i + 2]
            near = near + wym[i] * ym + wyp[i] * yp + wzm[i] * zm + wzp[i] * zp
            out.append(dg[i] * v[c] + coupled - near)
        return v, out

    def recv_rows(turn):
        return (
            lambda c, i: recv_y[turn, 0, 0, c, pl.ds(i, 1), :],
            lambda c, i: recv_y[turn, 1, 0, c, pl.ds(i, 1), :],
        )

    ghost_rows = (
        lambda c, i: gy[0, c, pl.ds(i, 1), :],
        lambda c, i: gy[1, c, pl.ds(i, 1), :],
    )

    def bcoef(k):
        return jnp.broadcast_to(coef[k : k + 1, :], (dy, dz))

    def ghost_weights(d, cross, low, high):
        near, far, bulk = [static_recv[d, k] for k in range(3)]
        inner = 0.5 * (near + far)
        across = 0.5 * (near + cross)
        rm, rp = rows_near(near, low, high)
        rm = 0.5 * (near + rm)
        rp = 0.5 * (near + rp)
        zm, zp = z_near(near)
        zm = 0.5 * (near + zm)
        zp = 0.5 * (near + zp)
        total = inner + across + rm + rp
        total = total + jnp.where(lane == dz - 1, near, zp) + jnp.where(lane == 0, near, zm)
        inv = jnp.where(has[d], 1.0, 0.0) / (total + 1.5 * bulk)
        zm = jnp.where(lane == 0, 0.0, zm)
        zp = jnp.where(lane == dz - 1, 0.0, zp)
        for k, value in enumerate(
            (inner, across, rm, rp, zm, zp, total + bulk, 0.5 * bulk, inv)
        ):
            ghost[d, k] = value

    def all_ghost_weights():
        def edge(inside, corner, at, own):
            return jnp.where(inside, recv_d[0, corner, at : at + 1, :], own)

        for d in range(4):
            s = d % 2
            near = static_recv[d, 0]
            ends = near[0:1], near[dy - 1 : dy]
            if d < 2:
                cross = (faces[0], s_send_up[...])[s]
                low = edge(has[2], 2 * s, 6, ends[0])
                high = edge(has[3], 2 * s + 1, 6, ends[1])
            else:
                cross = s_send_y[1 - s]
                low = edge(has[0], s, 7, ends[0])
                high = edge(has[1], 2 + s, 7, ends[1])
            ghost_weights(d, cross, low, high)

    def ghost_apply(d, v, inner, cross, low, high):
        w = [ghost[d, k] for k in range(9)]
        coupled = w[7] * (v[0] + v[1] + v[2])
        out = []
        for c in range(3):
            rm, rp = rows_near(v[c], low[c], high[c])
            zm, zp = z_near(v[c])
            near = w[0] * inner[c] + w[1] * cross[c] + w[2] * rm + w[3] * rp
            near = near + w[4] * zm + w[5] * zp
            out.append(w[8] * (w[6] * v[c] + coupled - near))
        return out

    def ghost_step(turn, other, update):
        for d in range(4):
            s = d % 2
            if d < 2:
                v = [nearest(turn, s, c) for c in range(3)]
                inner = [recv_x[turn, s, c, s] for c in range(3)]
                cross = [mixed[s, c] for c in range(3)]
                low = [recv_d[turn, 2 * s, c : c + 1, :] for c in range(3)]
                high = [recv_d[turn, 2 * s + 1, c : c + 1, :] for c in range(3)]
            else:
                v = [recv_y[turn, s, 0, c] for c in range(3)]
                inner = [recv_y[turn, s, 1, c] for c in range(3)]
                cross = [y_send[turn, 1 - s, 0, c] for c in range(3)]
                low = [recv_d[turn, s, 3 + c : 4 + c, :] for c in range(3)]
                high = [recv_d[turn, 2 + s, 3 + c : 4 + c, :] for c in range(3)]
            out = ghost_apply(d, v, inner, cross, low, high)
            for c in range(3):
                new = update(d, c, v[c], out[c])
                if d < 2:
                    u[other, c, (dx + 1) * s] = permute(new, 2 - s)
                else:
                    gy[s, c] = new

    def ring_start(own, store, ssem, rsem, peer_of, count, mine):
        copies = []
        for k in range(1, count):
            copies.append(remote(own, store.at[k], ssem.at[k], rsem.at[k], peer_of(k)))
        for copy in copies:
            copy.start()
        return copies

    group_peer = lambda k: (b, lax.rem(g + k, ng))
    brick_peer = lambda k: (lax.rem(b + k, nb), g)

    m_copies = ring_start(m_own, m_all, m_ssem, m_rsem, group_peer, ng, g)
    top = m_own[...]
    for k, copy in enumerate(m_copies):
        copy.wait()
        top = jnp.maximum(top, m_all[k + 1])
    m2_own[...] = top
    m2_copies = ring_start(m2_own, m2_all, m2_ssem, m2_rsem, brick_peer, nb, b)
    exchange_wait(t_copy)

    low, high = recv_rows(0)

    def first_plane(i, _):
        _, out = apply_plane(i, 0, low, high)
        inv = invd[i]
        for c in range(3):
            r[c, i] = out[c]
            u[1, c, i + 1] = out[c] * inv
        return 0

    def first_ghosts():
        all_ghost_weights()

        def update(d, c, v, out):
            before[d, c] = out
            return out

        ghost_step(0, 1, update)

    sweep_receive(first_plane, 0, 0, 0, first_ghosts)

    def second_plane(i, _):
        _, out = apply_plane(i, 1, *ghost_rows)
        for c in range(3):
            res[c, i] = out[c]
        return 0

    lax.fori_loop(0, dx, second_plane, 0, unroll=8)

    for k, copy in enumerate(m2_copies):
        copy.wait()
        top = jnp.maximum(top, m2_all[k + 1])
    upper = BOUND_MARGIN * jnp.broadcast_to(jnp.max(top, axis=1, keepdims=True), top.shape)
    lower = LOW_RATIO * upper
    theta = 0.5 * (upper + lower)
    delta = 0.5 * (upper - lower)
    sigma = theta / delta
    damping = 1.0 / sigma
    inv_theta = 1.0 / theta
    coef[0:8] = inv_theta
    rows = []
    for turn in range(1, CHEB):
        following = 1.0 / (2.0 * sigma - damping)
        rows.append((following * damping, 2.0 * following / delta))
        damping = following
    for turn, (a, c2) in enumerate(rows):
        coef[8 + 2 * turn : 9 + 2 * turn] = a[0:1]
        coef[9 + 2 * turn : 10 + 2 * turn] = c2[0:1]
    coef[14:15] = (rows[0][0] * inv_theta + rows[0][1])[0:1]
    coef[15:16] = (rows[0][1] * inv_theta)[0:1]
    for k in range(CHEB - 2):
        (a, c2), (a_next, c_next) = rows[k], rows[k + 1]
        ratio = c_next / c2
        coef[16 + 2 * k : 17 + 2 * k] = (a_next + ratio)[0:1]
        coef[17 + 2 * k : 18 + 2 * k] = (ratio * a)[0:1]

    alpha, beta, it = bcoef(14), bcoef(15), bcoef(0)
    both_it = alpha + it
    a_two, c_two = bcoef(10), bcoef(11)

    def combine_plane(i, _):
        inv = invd[i]
        for c in range(3):
            d0 = u[0, c, i + 1]
            one = alpha * d0 - beta * u[1, c, i + 1]
            sol[c, i] = it * d0 + one
            rest = rhs[c, i] - both_it * r[c, i] + beta * res[c, i]
            res[c, i] = rest
            two = a_two * one + c_two * (rest * inv)
            u[0, c, i + 1] = two
            store_rows(1, c, i, two)
        return 0

    sweep_send(combine_plane, 1, 0, 0)
    for d in range(4):
        for c in range(3):
            v = nearest(0, d, c) if d < 2 else recv_y[0, d - 2, 0, c]
            before[d, c] = alpha * v - beta * before[d, c]

    def step_plane(slot, low, high, a, c2, following, summed=False, rows_of=None):
        other = 1 - slot

        def plane(i, sums):
            v, out = apply_plane(i, slot, low, high)
            inv = invd[i]
            new = []
            for c in range(3):
                rest = res[c, i] - out[c]
                res[c, i] = rest
                sol[c, i] = sol[c, i] + v[c]
                if summed:
                    new.append(sums[c] + rest)
                if not following:
                    continue
                ahead = c2 * (rest * inv)
                if a is not None:
                    ahead = ahead + a * v[c]
                u[other, c, i + 1] = ahead
                if rows_of is not None:
                    store_rows(rows_of, c, i, ahead)
            return tuple(new)
        return plane

    def pair_ghosts(turn, other, k):
        def done():
            e1, e2, e3 = bcoef(16 + 2 * k), bcoef(17 + 2 * k), bcoef(11 + 2 * k)

            def update(d, c, v, out):
                return e1 * v - e2 * before[d, c] - e3 * out

            ghost_step(turn, other, update)
        return done

    def i_copy(d):
        return remote(inverse, inv_recv.at[d], i_ssem.at[d], i_rsem.at[d], peers[d])

    exchange_start(i_copy, (0, 1))
    plane = step_plane(0, *recv_rows(1), bcoef(12), bcoef(13), True)
    sweep_receive(plane, 1, 0, (), pair_ghosts(1, 1, 1))
    plane = step_plane(1, *ghost_rows, None, bcoef(0), True, summed=True, rows_of=2)
    init = tuple(jnp.zeros((dy, dz), jnp.float32) for _ in range(3))
    sums = sweep_send(plane, 2, 0, init)

    c_own[...] = jnp.zeros(c_own.shape, jnp.float32)
    for c in range(3):
        c_own[c : c + 1, :] = jnp.sum(sums[c], axis=0, keepdims=True)
    c_all[1, g] = c_own[...]

    def c_copy(q, k):
        slot = q * ng + k
        return remote(
            c_own, c_all.at[q, g], c_ssem.at[slot], c_rsem.at[slot],
            (b + 1 - q, lax.rem(g + k, ng)),
        )

    def c_arrival(q, k):
        slot = q * ng + k
        source = lax.rem(g + ng - k, ng)
        return remote(
            c_own, c_all.at[q, source], c_ssem.at[slot], c_rsem.at[slot],
            (b + 1 - q, lax.rem(g + k, ng)),
        )

    def coarse_all(to_do, flags):
        for q in (0, 2, 1):
            first = 1 if q == 1 else 0
            if q == 1:
                for k in range(first, ng):
                    to_do(q, k)
                continue

            @pl.when(flags[q])
            def _():
                for k in range(first, ng):
                    to_do(q, k)

    coarse_all(lambda q, k: c_copy(q, k).start(), {0: has[1], 2: has[0]})
    f_all[...] = jnp.zeros(f_all.shape, jnp.float32)
    exchange_wait(i_copy, (0, 1))
    coarse_all(lambda q, k: c_arrival(q, k).wait_recv(), {0: has[0], 2: has[1]})
    coarse_all(lambda q, k: c_copy(q, k).wait_send(), {0: has[1], 2: has[0]})

    cells_z = dz // BLOCK_Z
    size = 3 * cells_z * ng
    flat = c_all[...].reshape(3 * ng * 8, dz)
    li = lax.broadcasted_iota(jnp.int32, (dz, size), 0)
    ki = lax.broadcasted_iota(jnp.int32, (dz, size), 1)
    gather = jnp.where(li // BLOCK_Z == ki % cells_z, 1.0 / (dx * dy * BLOCK_Z), 0.0)
    spread = jnp.dot(flat, gather, precision=HIGHEST, preferred_element_type=jnp.float32)
    ri = lax.broadcasted_iota(jnp.int32, (ng * 8, size), 0)
    kk = lax.broadcasted_iota(jnp.int32, (ng * 8, size), 1) // cells_z
    mine = (ri // 8 == kk // 3) & (ri % 8 == kk % 3)
    bi = lax.broadcasted_iota(jnp.int32, (size, dz), 0)
    bl = lax.broadcasted_iota(jnp.int32, (size, dz), 1)
    placed = bi % cells_z == bl // BLOCK_Z
    for q in range(3):
        part = spread[q * ng * 8 : (q + 1) * ng * 8]
        vector = jnp.sum(jnp.where(mine, part, 0.0), axis=0, keepdims=True)
        matrix = inverse[...] if q == 1 else inv_recv[q // 2]
        correction = jnp.sum(matrix * vector, axis=1, keepdims=True)
        table = jnp.where(placed, jnp.broadcast_to(correction, (size, dz)), 0.0)
        for k in range(ng):
            for c in range(3):
                start = (k * 3 + c) * cells_z
                f_all[q, k + 1, c : c + 1, :] = jnp.sum(
                    table[start : start + cells_z], axis=0, keepdims=True
                )

    def full(q, at, c):
        return jnp.broadcast_to(f_all[q, at, c : c + 1, :], (dy, dz))

    own_fine = [full(1, g + 1, c) for c in range(3)]

    def fill_plane(i, _):
        for c in range(3):
            u[1, c, i + 1] = own_fine[c]
        return 0

    lax.fori_loop(0, dx, fill_plane, 0, unroll=UNROLL)
    for c in range(3):
        u[1, c, 0] = full(0, g + 1, c)
        u[1, c, dx + 1] = full(2, g + 1, c)
    exchange_wait(h_copy(2, 0))
    plane = step_plane(
        1,
        lambda c, i: f_all[1, g, c : c + 1, :],
        lambda c, i: f_all[1, g + 2, c : c + 1, :],
        None,
        bcoef(0),
        True,
    )
    lax.fori_loop(0, dx, plane, (), unroll=8)

    it = bcoef(0)
    for d in range(4):
        s = d % 2
        if d < 2:
            q = 2 * s
            here = [full(q, g + 1, c) for c in range(3)]
            low = [f_all[q, g, c : c + 1, :] for c in range(3)]
            high = [f_all[q, g + 2, c : c + 1, :] for c in range(3)]
        else:
            at = g + 2 * s
            here = [full(1, at, c) for c in range(3)]
            low = [f_all[0, at, c : c + 1, :] for c in range(3)]
            high = [f_all[2, at, c : c + 1, :] for c in range(3)]
        out = ghost_apply(d, here, here, own_fine, low, high)
        for c in range(3):
            value = nearest(2, s, c) if d < 2 else recv_y[2, s, 0, c]
            value = value - it * out[c]
            before[d, c] = value
            if d < 2:
                u[0, c, (dx + 1) * s] = permute(value, 2 - s)
            else:
                gy[s, c] = value

    plane = step_plane(0, *ghost_rows, bcoef(8), bcoef(9), True, rows_of=3)
    sweep_send(plane, 3, 1, ())
    plane = step_plane(1, *recv_rows(3), bcoef(10), bcoef(11), True)
    sweep_receive(plane, 3, 1, (), pair_ghosts(3, 0, 0))
    plane = step_plane(0, *ghost_rows, bcoef(12), bcoef(13), True, rows_of=4)
    sweep_send(plane, 4, 1, ())
    plane = step_plane(1, *recv_rows(4), None, None, False)
    sweep_receive(plane, 4, 1, ())


def per_device(rhs, material, level, mortar, mu, lam, inverse):
    nb = lax.axis_size("bricks")
    ng = lax.axis_size("group")
    dx, dy, dz = material.shape
    f32 = jnp.float32
    vmem = pl.BlockSpec(memory_space=pltpu.VMEM)
    smem = pl.BlockSpec(memory_space=pltpu.SMEM)
    hbm = pl.BlockSpec(memory_space=pltpu.HBM)
    dma = pltpu.SemaphoreType.DMA
    grid = pltpu.VMEM((dx, dy, dz), f32)
    cg = inverse.shape[1]
    scratch = [
        pltpu.VMEM((3, dx, dy, dz), f32),
        pltpu.VMEM((dx, dy, dz), jnp.int32),
        pltpu.VMEM((cg, cg), f32),
        pltpu.VMEM((2, 3, dx + 2, dy, dz), f32),
        pltpu.VMEM((3, dx, dy, dz), f32),
        pltpu.VMEM((dx + 2, dy, dz), f32),
        pltpu.VMEM((dx + 1, dy, dz), f32),
        grid, grid, grid, grid, grid, grid, grid,
        pltpu.VMEM((24, dz), f32),
        pltpu.VMEM((dy, dz), f32),
        pltpu.VMEM((2, dx, dz), f32),
        pltpu.VMEM((4, dx, dz), f32),
        pltpu.VMEM((4, 3, dx, dz), f32),
        pltpu.VMEM((4, 3, dx, dz), f32),
        pltpu.VMEM((dy, dz), jnp.int32),
        pltpu.VMEM((dy, dz), jnp.int32),
        pltpu.VMEM((4, dy, dz), jnp.int32),
        pltpu.VMEM((1, dy, dz), f32),
        pltpu.VMEM((2, 3, dy, dz), f32),
        pltpu.VMEM((ROUNDS, 2, 2, 3, dx, dz), f32),
        pltpu.VMEM((ROUNDS, 4, 8, dz), f32),
        pltpu.VMEM((ROUNDS, 2, 3, 2, dy, dz), f32),
        pltpu.VMEM((ROUNDS, 2, 2, 3, dx, dz), f32),
        pltpu.VMEM((ROUNDS, 4, 8, dz), f32),
        pltpu.VMEM((4, 9, dy, dz), f32),
        pltpu.VMEM((2, 3, dx, dz), f32),
        pltpu.VMEM((4, 3, dy, dz), f32),
        pltpu.VMEM((8, dz), f32),
        pltpu.VMEM((ng, 8, dz), f32),
        pltpu.VMEM((8, dz), f32),
        pltpu.VMEM((nb, 8, dz), f32),
        pltpu.VMEM((8, dz), f32),
        pltpu.VMEM((3, ng, 8, dz), f32),
        pltpu.VMEM((3, ng + 2, 8, dz), f32),
        pltpu.VMEM((2, cg, cg), f32),
        dma((3,)),
        dma((4,)), dma((4,)),
        dma((5,)), dma((5,)),
        dma((ROUNDS, 8)), dma((ROUNDS, 8)),
        dma((ng,)), dma((ng,)),
        dma((nb,)), dma((nb,)),
        dma((3 * ng,)), dma((3 * ng,)),
        dma((2,)), dma((2,)),
    ]
    rhs, material, inverse, mortar, mu, lam = (
        pltpu.with_memory_space_constraint(x, pltpu.HBM)
        for x in (rhs, material, inverse, mortar, mu, lam)
    )
    return pl.pallas_call(
        functools.partial(kernel, nb, ng, dx, dy, dz),
        out_shape=(
            jax.ShapeDtypeStruct(rhs.shape, f32),
            jax.ShapeDtypeStruct(rhs.shape, f32),
        ),
        in_specs=[hbm, hbm, vmem, smem, smem, smem, hbm],
        out_specs=(vmem, vmem),
        scratch_shapes=scratch,
        compiler_params=pltpu.CompilerParams(
            collective_id=0, has_side_effects=True, vmem_limit_bytes=16 * 2**20
        ),
    )(rhs, material, level, mortar, mu, lam, inverse)


def solution(mesh):
    return jax.shard_map(
        per_device,
        mesh=mesh,
        in_specs=(
            P(None, "bricks", "group", None),
            P("bricks", "group", None),
            P("bricks", "group"),
            P("bricks", "group", None),
            P(),
            P(),
            P("bricks", None, None),
        ),
        out_specs=(P(None, "bricks", "group", None), P(None, "bricks", "group", None)),
        check_vma=False,
    )
```

time: 43.3 us -> 37.3 us (0.86)
  Pallas kernels: 40.4 us -> 34.4 us
    pallas_call x1, Pallas kernels: 40.4 us -> 34.4 us  [per_device(): pl.pallas_call(functools.partial(kernel, nb, ng, dx, dy, dz), out_shape=(...]
where the time goes in v1:
time: 37.3 us; the launch traced here: 37.1 us
  Pallas kernels  34.4 us (92%)
  local copies, waits for them, and re-layouts  1.49 us (4%)
  between operations  1.29 us (3%)
    pallas_call x1, Pallas kernels, per_device(): pl.pallas_call(functools.partial(kernel, nb, ng, dx, dy, dz), out_shape=(...  34.4 us
    unnamed x2, local copies, waits for them, and re-layouts  1.49 us

profile of v1, /device:TPU:0, one launch (start us, length us, event | category | flops | bytes accessed | tf_op | source)
XLA Modules:
  0.0 37.1 jit_solution(5574243468486462251)
XLA Ops:
  1.3 34.4 %shard_map.86 = (f32[3,16,16,128]{3,2,1,0:T(8,128)S(1)}, f32[3,16,16,128]{3,2,1,0:T(8,128)S(1)}) custom-call(f32[3,16,16,128]{3,2,1,0:T(8,128)} %rhs_in.1, s32[16,16,128]{2,1,0:T(8,128)} %material_in.1, s32[1,1]{1,0:T(1,128)S(6)} %copy.11.level, s32[1,1,16]{2,1,0:T(1,128)} %mortar.1, f32[4]{0:T(128)} %mu.1, f32[4]{0:T(128)} %lam.1, f32[1,48,48]{2,1,0:T(8,128)} %inverse_in.1), custom_call_target="tpu_custom_call" | custom-call | tf_op jit(solution)/shard_map/pallas_call | solution.py:818
  35.7 0.7 %copy.12 = f32[3,16,16,128]{3,2,1,0:T(8,128)} copy(f32[3,16,16,128]{3,2,1,0:T(8,128)S(1)} %get-tuple-element.4) | data formatting | bytes 786432
  36.4 0.7 %copy.13 = f32[3,16,16,128]{3,2,1,0:T(8,128)} copy(f32[3,16,16,128]{3,2,1,0:T(8,128)S(1)} %get-tuple-element.5) | data formatting | bytes 786432

commit v2 on v1

--- a/solution.py
+++ b/solution.py
@@ -11,9 +11,9 @@
 CHEB = 4
 LOW_RATIO = 0.15
 BOUND_MARGIN = 1.1
-ROUNDS = 5
-DEPTH = (2, 2, 1, 2, 1)
+ROUNDS = 4
 UNROLL = 4
+DEPTH = 2
 SWEEP = 7
 INNER = 6
 HIGHEST = lax.Precision.HIGHEST
@@ -26,8 +26,9 @@
     u, r, shear, wx, wyp, wym, wzp, wzm, dg, hb, invd, coef,
     s_send_up, s_send_y, s_recv, static_send, static_recv, index_send, index_recv, index,
     faces, mixed, y_send, corner_send, recv_x, recv_y, recv_d, ghost, gy, before,
+    pack_send, pack_recv, corner_pack, recv_k, corner_rows, spread_k,
     m_own, m_all, m2_own, m2_all, c_own, c_all, f_all, inv_recv, in_sem,
-    s_ssem, s_rsem, t_ssem, t_rsem, h_ssem, h_rsem,
+    s_ssem, s_rsem, t_ssem, t_rsem, h_ssem, h_rsem, p_ssem, p_rsem,
     m_ssem, m_rsem, m2_ssem, m2_rsem, c_ssem, c_rsem, i_ssem, i_rsem,
 ):
     b = lax.axis_index("bricks")
@@ -186,6 +187,7 @@
             one = jnp.ones((dy, dz), jnp.float32)
             for k in range(3):
                 static_recv[d, k] = one
+                pack_recv[d, k] = zero_face
             for turn in range(ROUNDS):
                 for c in range(3):
                     for j in range(2):
@@ -201,8 +203,8 @@
         @pl.when(jnp.logical_not(has_corner[k]))
         def _():
             for turn in range(ROUNDS):
-                if DEPTH[turn] == 2:
-                    recv_d[turn, k] = jnp.zeros(recv_d.shape[2:], jnp.float32)
+                recv_d[turn, k] = jnp.zeros(recv_d.shape[2:], jnp.float32)
+            recv_k[k] = jnp.zeros(recv_k.shape[1:], jnp.float32)
 
     fetch(1).wait()
     fetch(2).wait()
@@ -228,7 +230,7 @@
         return pltpu.roll(v, 1, 1), pltpu.roll(v, dz - 1, 1)
 
     def h_copy(turn, slot):
-        deep = DEPTH[turn]
+        deep = DEPTH
 
         def copy(d):
             if d == 0:
@@ -270,8 +272,6 @@
         def _():
             copy(1).start()
 
-        if DEPTH[turn] == 1:
-            return
         for c in range(3):
             bottom, top = u[slot, c, 1], u[slot, c, dx]
             mixed_low, mixed_high = permute(bottom, 3), permute(top, 0)
@@ -293,9 +293,8 @@
     def store_rows(turn, c, i, value):
         y_send[turn, 0, 0, c, pl.ds(i, 1), :] = value[dy - 1 : dy]
         y_send[turn, 1, 0, c, pl.ds(i, 1), :] = value[0:1]
-        if DEPTH[turn] == 2:
-            y_send[turn, 0, 1, c, pl.ds(i, 1), :] = value[dy - 2 : dy - 1]
-            y_send[turn, 1, 1, c, pl.ds(i, 1), :] = value[1:2]
+        y_send[turn, 0, 1, c, pl.ds(i, 1), :] = value[dy - 2 : dy - 1]
+        y_send[turn, 1, 1, c, pl.ds(i, 1), :] = value[1:2]
 
     def corners_wait(turn):
         for k in range(4):
@@ -316,25 +315,21 @@
             u[slot, c, dx + 1] = permute(nearest(turn, 1, c), 1)
 
     def sweep_send(plane, turn, slot, carry):
-        deep = DEPTH[turn]
-        for i in range(deep):
+        for i in range(DEPTH):
             carry = plane(i, carry)
             carry = plane(dx - 1 - i, carry)
         send_faces(turn, slot)
-        unroll = INNER if deep == 2 else SWEEP
-        carry = lax.fori_loop(deep, dx - deep, plane, carry, unroll=unroll)
+        carry = lax.fori_loop(DEPTH, dx - DEPTH, plane, carry, unroll=INNER)
         send_rows(turn, slot)
         return carry
 
-    def sweep_receive(plane, turn, slot, carry, faces_done=None):
+    def sweep_receive(plane, turn, slot, carry, faces_done):
         exchange_wait(h_copy(turn, slot), (2, 3))
         carry = lax.fori_loop(1, dx - 1, plane, carry, unroll=SWEEP)
         exchange_wait(h_copy(turn, slot), (0, 1))
-        if DEPTH[turn] == 2:
-            corners_wait(turn)
+        corners_wait(turn)
         place_faces(turn, slot)
-        if faces_done is not None:
-            faces_done()
+        faces_done()
         carry = plane(0, carry)
         carry = plane(dx - 1, carry)
         return carry
@@ -507,6 +502,49 @@
         top = jnp.maximum(top, m_all[k + 1])
     m2_own[...] = top
     m2_copies = ring_start(m2_own, m2_all, m2_ssem, m2_rsem, brick_peer, nb, b)
+
+    for d in range(2):
+        i = (dx - 2, 1)[d]
+        pack_send[d, 0] = invd[i]
+        pack_send[d, 1] = hb[i]
+        pack_send[d, 2] = jnp.where(row == 0, wym[i], jnp.where(row == dy - 1, wyp[i], 0.0))
+    for d, y in ((2, dy - 2), (3, 1)):
+        pack_send[d, 2] = zero_face
+        pack_send[d, 2, 0:1, :] = wx[0, y : y + 1, :]
+        pack_send[d, 2, dx - 1 : dx, :] = wx[dx, y : y + 1, :]
+        for i in range(dx):
+            pack_send[d, 0, i : i + 1, :] = invd[i, y : y + 1, :]
+            pack_send[d, 1, i : i + 1, :] = hb[i, y : y + 1, :]
+    for sx in range(2):
+        i = (dx - 1) * sx
+        values = (
+            invd[i], hb[i], wx[dx * sx],
+            jnp.where(row == 0, wym[i], 0.0), jnp.where(row == dy - 1, wyp[i], 0.0),
+            shear[i + 1],
+        )
+        for k, value in enumerate(values):
+            other = permute(value, (3, 0)[sx])
+            for sy in range(2):
+                y = (dy - 1) * sy
+                corner_pack[2 * sx + sy, k : k + 1, :] = value[y : y + 1]
+                corner_pack[2 * sx + sy, 8 + k : 9 + k, :] = other[y : y + 1]
+
+    def p_copy(d):
+        return remote(
+            pack_send.at[d], pack_recv.at[d], p_ssem.at[d], p_rsem.at[d], peers[d]
+        )
+
+    def k_copy(k, at):
+        return remote(
+            corner_pack.at[k], recv_k.at[at], p_ssem.at[4 + k], p_rsem.at[4 + at],
+            corner_peer[k],
+        )
+
+    exchange_start(p_copy)
+    for k in range(4):
+        @pl.when(has_corner[k])
+        def _():
+            k_copy(k, 3 - k).start()
     exchange_wait(t_copy)
 
     low, high = recv_rows(0)
@@ -559,11 +597,11 @@
         coef[9 + 2 * turn : 10 + 2 * turn] = c2[0:1]
     coef[14:15] = (rows[0][0] * inv_theta + rows[0][1])[0:1]
     coef[15:16] = (rows[0][1] * inv_theta)[0:1]
-    for k in range(CHEB - 2):
-        (a, c2), (a_next, c_next) = rows[k], rows[k + 1]
-        ratio = c_next / c2
-        coef[16 + 2 * k : 17 + 2 * k] = (a_next + ratio)[0:1]
-        coef[17 + 2 * k : 18 + 2 * k] = (ratio * a)[0:1]
+    (a, c2), (a_next, c_next) = rows[1], rows[2]
+    ratio = c_next / c2
+    coef[16:17] = (a_next + ratio)[0:1]
+    coef[17:18] = (ratio * a)[0:1]
+    coef[18:19] = (rows[0][0] + rows[0][1] * theta)[0:1]
 
     alpha, beta, it = bcoef(14), bcoef(15), bcoef(0)
     both_it = alpha + it
@@ -612,9 +650,9 @@
             return tuple(new)
         return plane
 
-    def pair_ghosts(turn, other, k):
+    def pair_ghosts(turn, other):
         def done():
-            e1, e2, e3 = bcoef(16 + 2 * k), bcoef(17 + 2 * k), bcoef(11 + 2 * k)
+            e1, e2, e3 = bcoef(16), bcoef(17), bcoef(13)
 
             def update(d, c, v, out):
                 return e1 * v - e2 * before[d, c] - e3 * out
@@ -627,7 +665,7 @@
 
     exchange_start(i_copy, (0, 1))
     plane = step_plane(0, *recv_rows(1), bcoef(12), bcoef(13), True)
-    sweep_receive(plane, 1, 0, (), pair_ghosts(1, 1, 1))
+    sweep_receive(plane, 1, 0, (), pair_ghosts(1, 1))
     plane = step_plane(1, *ghost_rows, None, bcoef(0), True, summed=True, rows_of=2)
     init = tuple(jnp.zeros((dy, dz), jnp.float32) for _ in range(3))
     sums = sweep_send(plane, 2, 0, init)
@@ -667,6 +705,20 @@
 
     coarse_all(lambda q, k: c_copy(q, k).start(), {0: has[1], 2: has[0]})
     f_all[...] = jnp.zeros(f_all.shape, jnp.float32)
+    exchange_wait(p_copy)
+    for k in range(4):
+        @pl.when(has_corner[k])
+        def _():
+            k_copy(k, k).wait_recv()
+    for k in range(4):
+        @pl.when(has_corner[k])
+        def _():
+            k_copy(k, k).wait_send()
+    for k in range(4):
+        for n in range(6):
+            for side in range(2):
+                at = 2 * k + side
+                corner_rows[n, at : at + 1, :] = recv_k[k, 8 * side + n : 8 * side + n + 1, :]
     exchange_wait(i_copy, (0, 1))
     coarse_all(lambda q, k: c_arrival(q, k).wait_recv(), {0: has[0], 2: has[1]})
     coarse_all(lambda q, k: c_copy(q, k).wait_send(), {0: has[1], 2: has[0]})
@@ -702,57 +754,127 @@
 
     own_fine = [full(1, g + 1, c) for c in range(3)]
 
-    def fill_plane(i, _):
-        for c in range(3):
-            u[1, c, i + 1] = own_fine[c]
+    fine_sides = [z_near(own_fine[c]) for c in range(3)]
+    fine_rows = [
+        (
+            jnp.where(row == 0, full(1, g, c), own_fine[c]),
+            jnp.where(row == dy - 1, full(1, g + 2, c), own_fine[c]),
+        )
+        for c in range(3)
+    ]
+    fine_sum = own_fine[0] + own_fine[1] + own_fine[2]
+    it = bcoef(0)
+
+    def fine_plane(i, _):
+        inv = invd[i]
+        coupled = hb[i] * fine_sum
+        for c in range(3):
+            f = own_fine[c]
+            first, last = isinstance(i, int) and i == 0, isinstance(i, int) and i == dx - 1
+            xm = full(0, g + 1, c) if first else f
+            xp = full(2, g + 1, c) if last else f
+            near = wx[i] * xm + wx[i + 1] * xp
+            near = near + wym[i] * fine_rows[c][0] + wyp[i] * fine_rows[c][1]
+            near = near + wzm[i] * fine_sides[c][0] + wzp[i] * fine_sides[c][1]
+            rest = res[c, i] - (dg[i] * f + coupled - near)
+            res[c, i] = rest
+            sol[c, i] = sol[c, i] + f
+            ahead = it * (rest * inv)
+            u[0, c, i + 1] = ahead
+            y_send[2, 0, 0, c, pl.ds(i, 1), :] = ahead[dy - 1 : dy]
+            y_send[2, 1, 0, c, pl.ds(i, 1), :] = ahead[0:1]
         return 0
 
-    lax.fori_loop(0, dx, fill_plane, 0, unroll=UNROLL)
+    exchange_wait(h_copy(2, 0))
+    corners_wait(2)
+    fine_plane(0, 0)
+    fine_plane(dx - 1, 0)
+    lax.fori_loop(1, dx - 1, fine_plane, 0, unroll=SWEEP)
     for c in range(3):
-        u[1, c, 0] = full(0, g + 1, c)
-        u[1, c, dx + 1] = full(2, g + 1, c)
-    exchange_wait(h_copy(2, 0))
-    plane = step_plane(
-        1,
-        lambda c, i: f_all[1, g, c : c + 1, :],
-        lambda c, i: f_all[1, g + 2, c : c + 1, :],
-        None,
-        bcoef(0),
-        True,
-    )
-    lax.fori_loop(0, dx, plane, (), unroll=8)
-
-    it = bcoef(0)
+        mixed[0, c] = permute(u[0, c, 1], 3)
+        mixed[1, c] = permute(u[0, c, dx], 0)
+
+    def fine_far(here, low, high, inv, half, w_low, w_high, near, across=None):
+        lanes = lane[: near.shape[0]]
+        zm, zp = z_near(near)
+        zm = jnp.where(lanes == 0, 0.0, 0.5 * (near + zm))
+        zp = jnp.where(lanes == dz - 1, 0.0, 0.5 * (near + zp))
+        rim = jnp.where((lanes == 0) | (lanes == dz - 1), near, 0.0)
+        weight = 2.0 * half + w_low + w_high + zm + zp + rim
+        if across is not None:
+            weight = weight + across[0]
+        coupled = half * (here[0] + here[1] + here[2])
+        out = []
+        for c in range(3):
+            fm, fp = z_near(here[c])
+            value = weight * here[c] + coupled - zm * fm - zp * fp
+            value = value - w_low * low[c] - w_high * high[c]
+            if across is not None:
+                value = value - across[0] * across[1][c]
+            out.append(inv * value)
+        return out
+
     for d in range(4):
         s = d % 2
         if d < 2:
-            q = 2 * s
-            here = [full(q, g + 1, c) for c in range(3)]
-            low = [f_all[q, g, c : c + 1, :] for c in range(3)]
-            high = [f_all[q, g + 2, c : c + 1, :] for c in range(3)]
+            spots = (2 * s, g + 1), (2 * s, g), (2 * s, g + 2)
         else:
             at = g + 2 * s
-            here = [full(1, at, c) for c in range(3)]
-            low = [f_all[0, at, c : c + 1, :] for c in range(3)]
-            high = [f_all[2, at, c : c + 1, :] for c in range(3)]
+            spots = (1, at), (0, at), (2, at)
+        here, low, high = [[full(*spot, c) for c in range(3)] for spot in spots]
         out = ghost_apply(d, here, here, own_fine, low, high)
-        for c in range(3):
-            value = nearest(2, s, c) if d < 2 else recv_y[2, s, 0, c]
-            value = value - it * out[c]
-            before[d, c] = value
+        inv, half, rim = [pack_recv[d, k] for k in range(3)]
+        w_low = jnp.where(row == 0, rim, 0.0)
+        w_high = jnp.where(row == dy - 1, rim, 0.0)
+        far = fine_far(here, low, high, inv, half, w_low, w_high, static_recv[d, 1])
+        for c in range(3):
             if d < 2:
-                u[0, c, (dx + 1) * s] = permute(value, 2 - s)
+                recv_x[2, s, c, 1 - s] = nearest(2, s, c) - it * out[c]
+                recv_x[2, s, c, s] = recv_x[2, s, c, s] - it * far[c]
             else:
-                gy[s, c] = value
-
-    plane = step_plane(0, *ghost_rows, bcoef(8), bcoef(9), True, rows_of=3)
-    sweep_send(plane, 3, 1, ())
-    plane = step_plane(1, *recv_rows(3), bcoef(10), bcoef(11), True)
-    sweep_receive(plane, 3, 1, (), pair_ghosts(3, 0, 0))
-    plane = step_plane(0, *ghost_rows, bcoef(12), bcoef(13), True, rows_of=4)
-    sweep_send(plane, 4, 1, ())
-    plane = step_plane(1, *recv_rows(4), None, None, False)
-    sweep_receive(plane, 4, 1, ())
+                recv_y[2, s, 0, c] = recv_y[2, s, 0, c] - it * out[c]
+                recv_y[2, s, 1, c] = recv_y[2, s, 1, c] - it * far[c]
+
+    for k, (sx, sy) in enumerate(corners):
+        q, at = 2 * sx, g + 2 * sy
+        spots = (q, at), (q, jnp.maximum(at - 1, 0)), (q, jnp.minimum(at + 1, ng + 1)), (1, at)
+        for n, spot in enumerate(spots):
+            for c in range(3):
+                value = f_all[(*spot, slice(c, c + 1))]
+                spread_k[n, c, 2 * k : 2 * k + 1, :] = value
+                spread_k[n, c, 2 * k + 1 : 2 * k + 2, :] = value
+        for c in range(3):
+            for n in range(2):
+                at = 2 * k + n
+                spread_k[4, c, at : at + 1, :] = recv_d[2, k, 3 * n + c : 3 * n + c + 1, :]
+    here, low, high, beside = [[spread_k[n, c] for c in range(3)] for n in range(4)]
+    inv, half, cross, w_low, w_high, near = [corner_rows[n] for n in range(6)]
+    out = fine_far(here, low, high, inv, half, w_low, w_high, near, (cross, beside))
+    for c in range(3):
+        spread_k[4, c] = spread_k[4, c] - it[0:8] * out[c]
+    for k in range(4):
+        for c in range(3):
+            for n in range(2):
+                at = 2 * k + n
+                recv_d[2, k, 3 * n + c : 3 * n + c + 1, :] = spread_k[4, c, at : at + 1, :]
+
+    place_faces(2, 0)
+    e1, e3 = bcoef(18), bcoef(9)
+
+    def first_update(d, c, v, out):
+        new = e1 * v - e3 * out
+        before[d, c] = new
+        return new
+
+    ghost_step(2, 1, first_update)
+    plane = step_plane(0, *recv_rows(2), bcoef(8), bcoef(9), True)
+    lax.fori_loop(0, dx, plane, (), unroll=8)
+    plane = step_plane(1, *ghost_rows, bcoef(10), bcoef(11), True, rows_of=3)
+    sweep_send(plane, 3, 0, ())
+    plane = step_plane(0, *recv_rows(3), bcoef(12), bcoef(13), True)
+    sweep_receive(plane, 3, 0, (), pair_ghosts(3, 1))
+    plane = step_plane(1, *ghost_rows, None, None, False)
+    lax.fori_loop(0, dx, plane, (), unroll=8)
 
 
 def per_device(rhs, material, level, mortar, mu, lam, inverse):
@@ -794,6 +916,12 @@
         pltpu.VMEM((4, 9, dy, dz), f32),
         pltpu.VMEM((2, 3, dx, dz), f32),
         pltpu.VMEM((4, 3, dy, dz), f32),
+        pltpu.VMEM((4, 3, dx, dz), f32),
+        pltpu.VMEM((4, 3, dx, dz), f32),
+        pltpu.VMEM((4, 16, dz), f32),
+        pltpu.VMEM((4, 16, dz), f32),
+        pltpu.VMEM((6, 8, dz), f32),
+        pltpu.VMEM((5, 3, 8, dz), f32),
         pltpu.VMEM((8, dz), f32),
         pltpu.VMEM((ng, 8, dz), f32),
         pltpu.VMEM((8, dz), f32),
@@ -806,6 +934,7 @@
         dma((4,)), dma((4,)),
         dma((5,)), dma((5,)),
         dma((ROUNDS, 8)), dma((ROUNDS, 8)),
+        dma((8,)), dma((8,)),
         dma((ng,)), dma((ng,)),
         dma((nb,)), dma((nb,)),
         dma((3 * ng,)), dma((3 * ng,)),

time: 37.3 us -> 35.3 us (0.946); the launches traced: 37.1 us -> 34.8 us
  Pallas kernels: 34.4 us -> 32 us
    pallas_call x1, Pallas kernels: 34.4 us -> 32 us  [per_device(): pl.pallas_call(functools.partial(kernel, nb, ng, dx, dy, dz), out_shape=(...]
where the time goes in v2:
time: 35.3 us; the launch traced here: 34.8 us
  Pallas kernels  32 us (91%)
  local copies, waits for them, and re-layouts  1.49 us (4%)
  between operations  1.29 us (4%)
    pallas_call x1, Pallas kernels, per_device(): pl.pallas_call(functools.partial(kernel, nb, ng, dx, dy, dz), out_shape=(...  32 us
    unnamed x2, local copies, waits for them, and re-layouts  1.49 us

profile of v2, /device:TPU:0, one launch (start us, length us, event | category | flops | bytes accessed | tf_op | source)
XLA Modules:
  0.0 34.8 jit_solution(5698244978216040577)
XLA Ops:
  1.3 32.0 %shard_map.86 = (f32[3,16,16,128]{3,2,1,0:T(8,128)S(1)}, f32[3,16,16,128]{3,2,1,0:T(8,128)S(1)}) custom-call(f32[3,16,16,128]{3,2,1,0:T(8,128)} %rhs_in.1, s32[16,16,128]{2,1,0:T(8,128)} %material_in.1, s32[1,1]{1,0:T(1,128)S(6)} %copy.11.level, s32[1,1,16]{2,1,0:T(1,128)} %mortar.1, f32[4]{0:T(128)} %mu.1, f32[4]{0:T(128)} %lam.1, f32[1,48,48]{2,1,0:T(8,128)} %inverse_in.1), custom_call_target="tpu_custom_call" | custom-call | tf_op jit(solution)/shard_map/pallas_call | solution.py:947
  33.3 0.7 %copy.12 = f32[3,16,16,128]{3,2,1,0:T(8,128)} copy(f32[3,16,16,128]{3,2,1,0:T(8,128)S(1)} %get-tuple-element.4) | data formatting | bytes 786432
  34.0 0.7 %copy.13 = f32[3,16,16,128]{3,2,1,0:T(8,128)} copy(f32[3,16,16,128]{3,2,1,0:T(8,128)S(1)} %get-tuple-element.5) | data formatting | bytes 786432

commit v3 on v2

--- a/solution.py
+++ b/solution.py
@@ -47,9 +47,12 @@
         )
 
     barrier = pltpu.get_barrier_semaphore()
+    paired = nb % 2 == 0
+    stride = 2 if paired else 1
+    partner = b + 1 - 2 * lax.rem(b, 2)
     others = [(b, lax.rem(g + k, ng)) for k in range(1, ng)]
-    others += [(lax.rem(b + k, nb), g) for k in range(1, nb)]
-    around = [(lax.rem(g + k, ng)) for k in range(1, ng)]
+    others += [(lax.rem(b + k, nb), g) for k in range(stride, nb, stride)]
+    around = [lax.rem(g + k, ng) for k in range(0 if paired else 1, ng)]
     for peer in others:
         pl.semaphore_signal(
             barrier, inc=1, device_id=peer, device_id_type=pl.DeviceIdType.MESH
@@ -220,11 +223,19 @@
         shear[dx + 1] = shear[dx]
 
     def rows_near(v, low, high):
-        m = jnp.where(row == 0, jnp.broadcast_to(low, v.shape), pltpu.roll(v, 1, 0))
-        p = jnp.where(
-            row == dy - 1, jnp.broadcast_to(high, v.shape), pltpu.roll(v, dy - 1, 0)
-        )
-        return m, p
+        half = dy // 2
+        at = row[:half]
+        parts = [v[:half], v[half:]]
+        down = [pltpu.roll(part, 1, 0) for part in parts]
+        up = [pltpu.roll(part, half - 1, 0) for part in parts]
+        low = jnp.broadcast_to(low[:half], parts[0].shape)
+        high = jnp.broadcast_to(high[:half], parts[0].shape)
+        m = [jnp.where(at == 0, low, down[0]), jnp.where(at == 0, down[0], down[1])]
+        p = [
+            jnp.where(at == half - 1, up[1], up[0]),
+            jnp.where(at == half - 1, high, up[1]),
+        ]
+        return jnp.concatenate(m, axis=0), jnp.concatenate(p, axis=0)
 
     def z_near(v):
         return pltpu.roll(v, 1, 1), pltpu.roll(v, dz - 1, 1)
@@ -382,8 +393,24 @@
         corner_send[0, k, 6:7, :] = plane[y : y + 1]
         corner_send[0, k, 7:8, :] = other[y : y + 1]
 
-    best = sweep_send(weight_plane, 0, 0, jnp.zeros((dy, dz), jnp.float32))
+    best = jnp.zeros((dy, dz), jnp.float32)
+    best = lax.fori_loop(0, dx, weight_plane, best, unroll=UNROLL)
     m_own[...] = jnp.broadcast_to(jnp.max(best, axis=0, keepdims=True), m_own.shape)
+
+    def m_copy(k):
+        peer = (b if k < ng else partner, lax.rem(g + k, ng))
+        return remote(m_own, m_all.at[k], m_ssem.at[k], m_rsem.at[k], peer)
+
+    def m2_copy(k):
+        peer = (lax.rem(b + k * stride, nb), g)
+        return remote(m2_own, m2_all.at[k], m2_ssem.at[k], m2_rsem.at[k], peer)
+
+    m_copies = [m_copy(k) for k in range(1, 2 * ng if paired else ng)]
+    m2_copies = [m2_copy(k) for k in range(1, nb // stride)]
+    for copy in m_copies[::-1]:
+        copy.start()
+    send_faces(0, 0)
+    send_rows(0, 0)
 
     def apply_plane(i, slot, low, high):
         v = [u[slot, c, i + 1] for c in range(3)]
@@ -461,8 +488,9 @@
             out.append(w[8] * (w[6] * v[c] + coupled - near))
         return out
 
-    def ghost_step(turn, other, update):
-        for d in range(4):
+    def ghost_step(turn, other, update, directions=(0, 1, 2, 3), ends=True):
+        none = [jnp.zeros((1, dz), jnp.float32)] * 3
+        for d in directions:
             s = d % 2
             if d < 2:
                 v = [nearest(turn, s, c) for c in range(3)]
@@ -474,8 +502,10 @@
                 v = [recv_y[turn, s, 0, c] for c in range(3)]
                 inner = [recv_y[turn, s, 1, c] for c in range(3)]
                 cross = [y_send[turn, 1 - s, 0, c] for c in range(3)]
-                low = [recv_d[turn, s, 3 + c : 4 + c, :] for c in range(3)]
-                high = [recv_d[turn, 2 + s, 3 + c : 4 + c, :] for c in range(3)]
+                low, high = none, none
+                if ends:
+                    low = [recv_d[turn, s, 3 + c : 4 + c, :] for c in range(3)]
+                    high = [recv_d[turn, 2 + s, 3 + c : 4 + c, :] for c in range(3)]
             out = ghost_apply(d, v, inner, cross, low, high)
             for c in range(3):
                 new = update(d, c, v[c], out[c])
@@ -484,24 +514,13 @@
                 else:
                     gy[s, c] = new
 
-    def ring_start(own, store, ssem, rsem, peer_of, count, mine):
-        copies = []
-        for k in range(1, count):
-            copies.append(remote(own, store.at[k], ssem.at[k], rsem.at[k], peer_of(k)))
-        for copy in copies:
-            copy.start()
-        return copies
-
-    group_peer = lambda k: (b, lax.rem(g + k, ng))
-    brick_peer = lambda k: (lax.rem(b + k, nb), g)
-
-    m_copies = ring_start(m_own, m_all, m_ssem, m_rsem, group_peer, ng, g)
     top = m_own[...]
     for k, copy in enumerate(m_copies):
         copy.wait()
         top = jnp.maximum(top, m_all[k + 1])
     m2_own[...] = top
-    m2_copies = ring_start(m2_own, m2_all, m2_ssem, m2_rsem, brick_peer, nb, b)
+    for copy in m2_copies:
+        copy.start()
 
     for d in range(2):
         i = (dx - 2, 1)[d]
@@ -651,24 +670,38 @@
         return plane
 
     def pair_ghosts(turn, other):
-        def done():
+        def done(directions=(0, 1, 2, 3), ends=True):
             e1, e2, e3 = bcoef(16), bcoef(17), bcoef(13)
 
             def update(d, c, v, out):
                 return e1 * v - e2 * before[d, c] - e3 * out
 
-            ghost_step(turn, other, update)
+            ghost_step(turn, other, update, directions, ends)
         return done
+
+    def pair_receive(turn, slot, first, second, carry, ghosts):
+        exchange_wait(h_copy(turn, slot), (2, 3))
+        lax.fori_loop(1, dx - 1, first, (), unroll=SWEEP)
+        ghosts((2, 3), False)
+        carry = lax.fori_loop(2, dx - 2, second, carry, unroll=INNER)
+        exchange_wait(h_copy(turn, slot), (0, 1))
+        corners_wait(turn)
+        place_faces(turn, slot)
+        ghosts()
+        for i in (0, dx - 1):
+            first(i, ())
+        for i in (0, 1, dx - 2, dx - 1):
+            carry = second(i, carry)
+        return carry
 
     def i_copy(d):
         return remote(inverse, inv_recv.at[d], i_ssem.at[d], i_rsem.at[d], peers[d])
 
     exchange_start(i_copy, (0, 1))
-    plane = step_plane(0, *recv_rows(1), bcoef(12), bcoef(13), True)
-    sweep_receive(plane, 1, 0, (), pair_ghosts(1, 1))
-    plane = step_plane(1, *ghost_rows, None, bcoef(0), True, summed=True, rows_of=2)
+    first = step_plane(0, *recv_rows(1), bcoef(12), bcoef(13), True)
+    second = step_plane(1, *ghost_rows, None, bcoef(0), True, summed=True, rows_of=2)
     init = tuple(jnp.zeros((dy, dz), jnp.float32) for _ in range(3))
-    sums = sweep_send(plane, 2, 0, init)
+    sums = pair_receive(1, 0, first, second, init, pair_ghosts(1, 1))
 
     c_own[...] = jnp.zeros(c_own.shape, jnp.float32)
     for c in range(3):
@@ -704,6 +737,8 @@
                     to_do(q, k)
 
     coarse_all(lambda q, k: c_copy(q, k).start(), {0: has[1], 2: has[0]})
+    send_faces(2, 0)
+    send_rows(2, 0)
     f_all[...] = jnp.zeros(f_all.shape, jnp.float32)
     exchange_wait(p_copy)
     for k in range(4):
@@ -787,9 +822,9 @@
 
     exchange_wait(h_copy(2, 0))
     corners_wait(2)
-    fine_plane(0, 0)
-    fine_plane(dx - 1, 0)
-    lax.fori_loop(1, dx - 1, fine_plane, 0, unroll=SWEEP)
+    for i in range(4):
+        fine_plane(i, 0)
+        fine_plane(dx - 1 - i, 0)
     for c in range(3):
         mixed[0, c] = permute(u[0, c, 1], 3)
         mixed[1, c] = permute(u[0, c, dx], 0)
@@ -866,15 +901,24 @@
         before[d, c] = new
         return new
 
+    first = step_plane(0, *recv_rows(2), bcoef(8), bcoef(9), True)
+    second = step_plane(1, *ghost_rows, bcoef(10), bcoef(11), True, rows_of=3)
     ghost_step(2, 1, first_update)
-    plane = step_plane(0, *recv_rows(2), bcoef(8), bcoef(9), True)
-    lax.fori_loop(0, dx, plane, (), unroll=8)
-    plane = step_plane(1, *ghost_rows, bcoef(10), bcoef(11), True, rows_of=3)
-    sweep_send(plane, 3, 0, ())
-    plane = step_plane(0, *recv_rows(3), bcoef(12), bcoef(13), True)
-    sweep_receive(plane, 3, 0, (), pair_ghosts(3, 1))
-    plane = step_plane(1, *ghost_rows, None, None, False)
-    lax.fori_loop(0, dx, plane, (), unroll=8)
+    for i in range(3):
+        first(i, ())
+        first(dx - 1 - i, ())
+    for i in range(2):
+        second(i, ())
+        second(dx - 1 - i, ())
+    send_faces(3, 0)
+    lax.fori_loop(4, dx - 4, fine_plane, 0, unroll=8)
+    ghost_step(2, 1, first_update, (2, 3))
+    lax.fori_loop(3, dx - 3, first, (), unroll=5)
+    lax.fori_loop(2, dx - 2, second, (), unroll=INNER)
+    send_rows(3, 0)
+    first = step_plane(0, *recv_rows(3), bcoef(12), bcoef(13), True)
+    second = step_plane(1, *ghost_rows, None, None, False)
+    pair_receive(3, 0, first, second, (), pair_ghosts(3, 1))
 
 
 def per_device(rhs, material, level, mortar, mu, lam, inverse):
@@ -923,7 +967,7 @@
         pltpu.VMEM((6, 8, dz), f32),
         pltpu.VMEM((5, 3, 8, dz), f32),
         pltpu.VMEM((8, dz), f32),
-        pltpu.VMEM((ng, 8, dz), f32),
+        pltpu.VMEM((2 * ng, 8, dz), f32),
         pltpu.VMEM((8, dz), f32),
         pltpu.VMEM((nb, 8, dz), f32),
         pltpu.VMEM((8, dz), f32),
@@ -935,7 +979,7 @@
         dma((5,)), dma((5,)),
         dma((ROUNDS, 8)), dma((ROUNDS, 8)),
         dma((8,)), dma((8,)),
-        dma((ng,)), dma((ng,)),
+        dma((2 * ng,)), dma((2 * ng,)),
         dma((nb,)), dma((nb,)),
         dma((3 * ng,)), dma((3 * ng,)),
         dma((2,)), dma((2,)),

time: 35.3 us -> 34.1 us (0.966)
  Pallas kernels: 32 us -> 30.9 us
    pallas_call x1, Pallas kernels: 32 us -> 30.9 us  [per_device(): pl.pallas_call(functools.partial(kernel, nb, ng, dx, dy, dz), out_shape=(...]
where the time goes in v3:
time: 34.1 us; the launch traced here: 33.7 us
  Pallas kernels  30.9 us (91%)
  local copies, waits for them, and re-layouts  1.49 us (4%)
  between operations  1.29 us (4%)
    pallas_call x1, Pallas kernels, per_device(): pl.pallas_call(functools.partial(kernel, nb, ng, dx, dy, dz), out_shape=(...  30.9 us
    unnamed x2, local copies, waits for them, and re-layouts  1.49 us

profile of v3, /device:TPU:0, one launch (start us, length us, event | category | flops | bytes accessed | tf_op | source)
XLA Modules:
  0.0 33.7 jit_solution(3842028033452557061)
XLA Ops:
  1.3 30.9 %shard_map.86 = (f32[3,16,16,128]{3,2,1,0:T(8,128)S(1)}, f32[3,16,16,128]{3,2,1,0:T(8,128)S(1)}) custom-call(f32[3,16,16,128]{3,2,1,0:T(8,128)} %rhs_in.1, s32[16,16,128]{2,1,0:T(8,128)} %material_in.1, s32[1,1]{1,0:T(1,128)S(6)} %copy.11.level, s32[1,1,16]{2,1,0:T(1,128)} %mortar.1, f32[4]{0:T(128)} %mu.1, f32[4]{0:T(128)} %lam.1, f32[1,48,48]{2,1,0:T(8,128)} %inverse_in.1), custom_call_target="tpu_custom_call" | custom-call | tf_op jit(solution)/shard_map/pallas_call | solution.py:991
  32.2 0.7 %copy.12 = f32[3,16,16,128]{3,2,1,0:T(8,128)} copy(f32[3,16,16,128]{3,2,1,0:T(8,128)S(1)} %get-tuple-element.4) | data formatting | bytes 786432
  33.0 0.7 %copy.13 = f32[3,16,16,128]{3,2,1,0:T(8,128)} copy(f32[3,16,16,128]{3,2,1,0:T(8,128)S(1)} %get-tuple-element.5) | data formatting | bytes 786432

commit v4 on v3

--- a/solution.py
+++ b/solution.py
@@ -14,15 +14,15 @@
 ROUNDS = 4
 UNROLL = 4
 DEPTH = 2
-SWEEP = 7
-INNER = 6
+SWEEP = 14
+INNER = 12
 HIGHEST = lax.Precision.HIGHEST
 
 
 def kernel(
     nb, ng, dx, dy, dz,
     rhs_in, material_in, level, mortar, mu, lam, inverse_in,
-    sol, res, rhs, material, inverse,
+    result, rhs, material, inverse,
     u, r, shear, wx, wyp, wym, wzp, wzm, dg, hb, invd, coef,
     s_send_up, s_send_y, s_recv, static_send, static_recv, index_send, index_recv, index,
     faces, mixed, y_send, corner_send, recv_x, recv_y, recv_d, ghost, gy, before,
@@ -31,6 +31,7 @@
     s_ssem, s_rsem, t_ssem, t_rsem, h_ssem, h_rsem, p_ssem, p_rsem,
     m_ssem, m_rsem, m2_ssem, m2_rsem, c_ssem, c_rsem, i_ssem, i_rsem,
 ):
+    sol, res = result.at[0], result.at[1]
     b = lax.axis_index("bricks")
     g = lax.axis_index("group")
     has = [b > 0, b < nb - 1, g > 0, g < ng - 1]
@@ -283,6 +284,7 @@
         def _():
             copy(1).start()
 
+    def send_corners(turn, slot):
         for c in range(3):
             bottom, top = u[slot, c, 1], u[slot, c, dx]
             mixed_low, mixed_high = permute(bottom, 3), permute(top, 0)
@@ -330,6 +332,7 @@
             carry = plane(i, carry)
             carry = plane(dx - 1 - i, carry)
         send_faces(turn, slot)
+        send_corners(turn, slot)
         carry = lax.fori_loop(DEPTH, dx - DEPTH, plane, carry, unroll=INNER)
         send_rows(turn, slot)
         return carry
@@ -347,14 +350,6 @@
 
     wx[0] = 0.5 * (shear[0] + shear[1])
     wx[dx] = 0.5 * (shear[dx] + shear[dx + 1])
-
-    exchange_wait(t_copy, (4,))
-    index[2] = index_recv[...]
-    undo_below = jnp.zeros((dy, dz), jnp.int32)
-    for k in range(dy):
-        at = jnp.broadcast_to(index_recv[k : k + 1, :], (dy, dz))
-        undo_below = jnp.where(row == at, k, undo_below)
-    index[3] = undo_below
 
     def weight_plane(i, best):
         s = shear[i + 1]
@@ -384,6 +379,31 @@
             store_rows(0, c, i, d0)
         return jnp.maximum(best, (2.0 * total + 2.5 * bulk) / diagonal)
 
+    best = jnp.zeros((dy, dz), jnp.float32)
+    best = lax.fori_loop(0, dx, weight_plane, best, unroll=UNROLL)
+    m_own[...] = jnp.broadcast_to(jnp.max(best, axis=0, keepdims=True), m_own.shape)
+
+    def m_copy(k):
+        peer = (b if k < ng else partner, lax.rem(g + k, ng))
+        return remote(m_own, m_all.at[k], m_ssem.at[k], m_rsem.at[k], peer)
+
+    def m2_copy(k):
+        peer = (lax.rem(b + k * stride, nb), g)
+        return remote(m2_own, m2_all.at[k], m2_ssem.at[k], m2_rsem.at[k], peer)
+
+    m_copies = [m_copy(k) for k in range(1, 2 * ng if paired else ng)]
+    m2_copies = [m2_copy(k) for k in range(1, nb // stride)]
+    for copy in m_copies[::-1]:
+        copy.start()
+    send_faces(0, 0)
+    send_rows(0, 0)
+    exchange_wait(t_copy, (4,))
+    index[2] = index_recv[...]
+    undo_below = jnp.zeros((dy, dz), jnp.int32)
+    for k in range(dy):
+        at = jnp.broadcast_to(index_recv[k : k + 1, :], (dy, dz))
+        undo_below = jnp.where(row == at, k, undo_below)
+    index[3] = undo_below
     below_shear = permute(shear[1], 3)
     faces[0] = below_shear
     for k, (sx, sy) in enumerate(corners):
@@ -392,25 +412,7 @@
         other = (below_shear, s_send_up[...])[sx]
         corner_send[0, k, 6:7, :] = plane[y : y + 1]
         corner_send[0, k, 7:8, :] = other[y : y + 1]
-
-    best = jnp.zeros((dy, dz), jnp.float32)
-    best = lax.fori_loop(0, dx, weight_plane, best, unroll=UNROLL)
-    m_own[...] = jnp.broadcast_to(jnp.max(best, axis=0, keepdims=True), m_own.shape)
-
-    def m_copy(k):
-        peer = (b if k < ng else partner, lax.rem(g + k, ng))
-        return remote(m_own, m_all.at[k], m_ssem.at[k], m_rsem.at[k], peer)
-
-    def m2_copy(k):
-        peer = (lax.rem(b + k * stride, nb), g)
-        return remote(m2_own, m2_all.at[k], m2_ssem.at[k], m2_rsem.at[k], peer)
-
-    m_copies = [m_copy(k) for k in range(1, 2 * ng if paired else ng)]
-    m2_copies = [m2_copy(k) for k in range(1, nb // stride)]
-    for copy in m_copies[::-1]:
-        copy.start()
-    send_faces(0, 0)
-    send_rows(0, 0)
+    send_corners(0, 0)
 
     def apply_plane(i, slot, low, high):
         v = [u[slot, c, i + 1] for c in range(3)]
@@ -738,6 +740,7 @@
 
     coarse_all(lambda q, k: c_copy(q, k).start(), {0: has[1], 2: has[0]})
     send_faces(2, 0)
+    send_corners(2, 0)
     send_rows(2, 0)
     f_all[...] = jnp.zeros(f_all.shape, jnp.float32)
     exchange_wait(p_copy)
@@ -911,6 +914,7 @@
         second(i, ())
         second(dx - 1 - i, ())
     send_faces(3, 0)
+    send_corners(3, 0)
     lax.fori_loop(4, dx - 4, fine_plane, 0, unroll=8)
     ghost_step(2, 1, first_update, (2, 3))
     lax.fori_loop(3, dx - 3, first, (), unroll=5)
@@ -988,19 +992,17 @@
         pltpu.with_memory_space_constraint(x, pltpu.HBM)
         for x in (rhs, material, inverse, mortar, mu, lam)
     )
-    return pl.pallas_call(
+    both = pl.pallas_call(
         functools.partial(kernel, nb, ng, dx, dy, dz),
-        out_shape=(
-            jax.ShapeDtypeStruct(rhs.shape, f32),
-            jax.ShapeDtypeStruct(rhs.shape, f32),
-        ),
+        out_shape=jax.ShapeDtypeStruct((2, *rhs.shape), f32),
         in_specs=[hbm, hbm, vmem, smem, smem, smem, hbm],
-        out_specs=(vmem, vmem),
+        out_specs=vmem,
         scratch_shapes=scratch,
         compiler_params=pltpu.CompilerParams(
             collective_id=0, has_side_effects=True, vmem_limit_bytes=16 * 2**20
         ),
     )(rhs, material, level, mortar, mu, lam, inverse)
+    return both[0], both[1]
 
 
 def solution(mesh):

time: 34.1 us -> 33.3 us (0.977)
  local copies, waits for them, and re-layouts: 1.49 us -> 0.96 us
    unnamed x2 -> x0, local copies, waits for them, and re-layouts: 1.49 us -> none
    squeeze x0 -> x1, local copies, waits for them, and re-layouts: none -> 0.96 us  [per_device(): return (both[0], both[1])]
where the time goes in v4:
time: 33.3 us; the launch traced here: 33.1 us
  Pallas kernels  30.8 us (92%)
  between operations  1.28 us (4%)
  local copies, waits for them, and re-layouts  0.96 us (3%)
    pallas_call x1, Pallas kernels, per_device(): pl.pallas_call(functools.partial(kernel, nb, ng, dx, dy, dz), out_shape=j...  30.8 us
    squeeze x1, local copies, waits for them, and re-layouts, per_device(): return (both[0], both[1])  0.96 us

profile of v4, /device:TPU:0, one launch (start us, length us, event | category | flops | bytes accessed | tf_op | source)
XLA Modules:
  0.0 33.1 jit_solution(6017177582512356929)
XLA Ops:
  1.3 30.8 %shard_map.86 = f32[2,3,16,16,128]{4,3,2,1,0:T(8,128)S(1)} custom-call(f32[3,16,16,128]{3,2,1,0:T(8,128)} %rhs_in.1, s32[16,16,128]{2,1,0:T(8,128)} %material_in.1, s32[1,1]{1,0:T(1,128)S(6)} %copy.9.level, s32[1,1,16]{2,1,0:T(1,128)} %mortar.1, f32[4]{0:T(128)} %mu.1, f32[4]{0:T(128)} %lam.1, f32[1,48,48]{2,1,0:T(8,128)} %inverse_in.1), custom_call_target="tpu_custom_call" | custom-call | tf_op jit(solution)/shard_map/pallas_call | solution.py:995
  32.1 1.0 %slice_bitcast_fusion = (f32[3,16,16,128]{3,2,1,0:T(8,128)}, f32[3,16,16,128]{3,2,1,0:T(8,128)}) fusion(f32[2,3,16,16,128]{4,3,2,1,0:T(8,128)S(1)} %shard_map.86), kind=kLoop, calls=%fused_computation | loop fusion | bytes 1572864 | tf_op jit(solution)/shard_map/squeeze | solution.py:1005

commit v5 on v4

--- a/solution.py
+++ b/solution.py
@@ -380,7 +380,7 @@
         return jnp.maximum(best, (2.0 * total + 2.5 * bulk) / diagonal)
 
     best = jnp.zeros((dy, dz), jnp.float32)
-    best = lax.fori_loop(0, dx, weight_plane, best, unroll=UNROLL)
+    best = lax.fori_loop(0, dx, weight_plane, best, unroll=16)
     m_own[...] = jnp.broadcast_to(jnp.max(best, axis=0, keepdims=True), m_own.shape)
 
     def m_copy(k):
@@ -595,7 +595,7 @@
             res[c, i] = out[c]
         return 0
 
-    lax.fori_loop(0, dx, second_plane, 0, unroll=8)
+    lax.fori_loop(0, dx, second_plane, 0, unroll=16)
 
     for k, copy in enumerate(m2_copies):
         copy.wait()
@@ -758,22 +758,22 @@
                 at = 2 * k + side
                 corner_rows[n, at : at + 1, :] = recv_k[k, 8 * side + n : 8 * side + n + 1, :]
     exchange_wait(i_copy, (0, 1))
-    coarse_all(lambda q, k: c_arrival(q, k).wait_recv(), {0: has[0], 2: has[1]})
-    coarse_all(lambda q, k: c_copy(q, k).wait_send(), {0: has[1], 2: has[0]})
-
     cells_z = dz // BLOCK_Z
     size = 3 * cells_z * ng
-    flat = c_all[...].reshape(3 * ng * 8, dz)
     li = lax.broadcasted_iota(jnp.int32, (dz, size), 0)
     ki = lax.broadcasted_iota(jnp.int32, (dz, size), 1)
     gather = jnp.where(li // BLOCK_Z == ki % cells_z, 1.0 / (dx * dy * BLOCK_Z), 0.0)
-    spread = jnp.dot(flat, gather, precision=HIGHEST, preferred_element_type=jnp.float32)
     ri = lax.broadcasted_iota(jnp.int32, (ng * 8, size), 0)
     kk = lax.broadcasted_iota(jnp.int32, (ng * 8, size), 1) // cells_z
     mine = (ri // 8 == kk // 3) & (ri % 8 == kk % 3)
     bi = lax.broadcasted_iota(jnp.int32, (size, dz), 0)
     bl = lax.broadcasted_iota(jnp.int32, (size, dz), 1)
     placed = bi % cells_z == bl // BLOCK_Z
+    coarse_all(lambda q, k: c_arrival(q, k).wait_recv(), {0: has[0], 2: has[1]})
+    coarse_all(lambda q, k: c_copy(q, k).wait_send(), {0: has[1], 2: has[0]})
+
+    flat = c_all[...].reshape(3 * ng * 8, dz)
+    spread = jnp.dot(flat, gather, precision=HIGHEST, preferred_element_type=jnp.float32)
     for q in range(3):
         part = spread[q * ng * 8 : (q + 1) * ng * 8]
         vector = jnp.sum(jnp.where(mine, part, 0.0), axis=0, keepdims=True)
@@ -823,11 +823,12 @@
             y_send[2, 1, 0, c, pl.ds(i, 1), :] = ahead[0:1]
         return 0
 
-    exchange_wait(h_copy(2, 0))
-    corners_wait(2)
+    sent_wait(h_copy(2, 0))
     for i in range(4):
         fine_plane(i, 0)
         fine_plane(dx - 1 - i, 0)
+    arrive_wait(h_copy(2, 0))
+    corners_wait(2)
     for c in range(3):
         mixed[0, c] = permute(u[0, c, 1], 3)
         mixed[1, c] = permute(u[0, c, dx], 0)
@@ -917,7 +918,7 @@
     send_corners(3, 0)
     lax.fori_loop(4, dx - 4, fine_plane, 0, unroll=8)
     ghost_step(2, 1, first_update, (2, 3))
-    lax.fori_loop(3, dx - 3, first, (), unroll=5)
+    lax.fori_loop(3, dx - 3, first, (), unroll=10)
     lax.fori_loop(2, dx - 2, second, (), unroll=INNER)
     send_rows(3, 0)
     first = step_plane(0, *recv_rows(3), bcoef(12), bcoef(13), True)

time: 33.3 us -> 32.9 us (0.988)
    pallas_call x1, Pallas kernels: 30.8 us -> 30.5 us  [per_device(): pl.pallas_call(functools.partial(kernel, nb, ng, dx, dy, dz), out_shape=j...]
where the time goes in v5:
time: 32.9 us; the launch traced here: 32.8 us
  Pallas kernels  30.5 us (93%)
  between operations  1.28 us (4%)
  local copies, waits for them, and re-layouts  0.96 us (3%)
    pallas_call x1, Pallas kernels, per_device(): pl.pallas_call(functools.partial(kernel, nb, ng, dx, dy, dz), out_shape=j...  30.5 us
    squeeze x1, local copies, waits for them, and re-layouts, per_device(): return (both[0], both[1])  0.96 us

profile of v5, /device:TPU:0, one launch (start us, length us, event | category | flops | bytes accessed | tf_op | source)
XLA Modules:
  0.0 32.8 jit_solution(11302482467494476599)
XLA Ops:
  1.3 30.5 %shard_map.86 = f32[2,3,16,16,128]{4,3,2,1,0:T(8,128)S(1)} custom-call(f32[3,16,16,128]{3,2,1,0:T(8,128)} %rhs_in.1, s32[16,16,128]{2,1,0:T(8,128)} %material_in.1, s32[1,1]{1,0:T(1,128)S(6)} %copy.9.level, s32[1,1,16]{2,1,0:T(1,128)} %mortar.1, f32[4]{0:T(128)} %mu.1, f32[4]{0:T(128)} %lam.1, f32[1,48,48]{2,1,0:T(8,128)} %inverse_in.1), custom_call_target="tpu_custom_call" | custom-call | tf_op jit(solution)/shard_map/pallas_call | solution.py:996
  31.8 1.0 %slice_bitcast_fusion = (f32[3,16,16,128]{3,2,1,0:T(8,128)}, f32[3,16,16,128]{3,2,1,0:T(8,128)}) fusion(f32[2,3,16,16,128]{4,3,2,1,0:T(8,128)S(1)} %shard_map.86), kind=kLoop, calls=%fused_computation | loop fusion | bytes 1572864 | tf_op jit(solution)/shard_map/squeeze | solution.py:1006
